TPU v7x, 256 devices: a whole 4x4x8 slice. The times are simulated.
256 devices in a mesh: cuts: 4 (over x), lat: 64 (over y, z, core).
Axes of the slice: x: 4, y: 4, z: 8, core: 2. Of those that a mesh axis runs over, the one named last changes fastest.
Arguments:
- object_contrast: float32 [2, 4, 8192, 4096], P(None, 'cuts', 'lat'), may hold values from -0.9 to 0.9
- probe: float32 [2, 256, 256], replicated, may hold values from -4.2 to 4.2
- intensity: float32 [256, 256, 256], P('lat'), may hold values from 0 to 3
- positions: int32 [256, 2], P('lat'), may hold values from -128 to 8064, as said below
- counts: int32 [64], P('lat'), may hold values from 1 to 4, as said below
Outputs:
- gradient: float32 [2, 4, 8192, 4096], P(None, 'cuts', 'lat')
Inputs may be any that keep to these rules, and one draw needn't show every extreme that they name: `positions`: position p = o * 4 + j belongs to lateral owner o. Its first entry is a multiple of 8 from (o - 1) * 128 to o * 128; its second entry is a multiple of 128 from 0 to 3840. Slots o * 4 + j with j >= counts[o] are unused. Owner 0 has 4 live positions in every draw.
All inputs are finite; a program needn't handle non-finite values.
Results may differ from a plain program's by a relative error of at most 0.0003.
Values sent between devices are 32-bit elements; how exact they have to be, the bound alone decides.
No kernel may reach another device: no remote copies, remote signals or barrier semaphores. Data moves between devices by JAX's collectives and lax.ppermute only.
A program may use at most 128 MiB of HBM per device.

v0:
```python
import math

import jax
import jax.numpy as jnp
import numpy as np
from jax import lax
from jax.experimental import pallas as pl
from jax.experimental.pallas import tpu as pltpu
from jax.sharding import PartitionSpec as P


PHASE_COEF = 64.0 * math.pi
VMEM = pl.BlockSpec(memory_space=pltpu.VMEM)
SMEM = pl.BlockSpec(memory_space=pltpu.SMEM)
HBM = pl.BlockSpec(memory_space=pltpu.HBM)
SMALL = pltpu.CompilerParams(vmem_limit_bytes=16 * 1024 * 1024)


def on_chip(shape, dtype=jnp.float32):
    return pltpu.VMEM(shape, dtype)


def chip(value):
    return pltpu.with_memory_space_constraint(value, pltpu.VMEM)


def off_chip(value):
    return pltpu.with_memory_space_constraint(value, pltpu.HBM)


def wave_tables(size):
    half = size // 2
    ticks = np.arange(size)
    freqs = np.where(ticks < half, ticks, ticks - size).astype(np.float64)
    turns = (ticks[:, None] * ticks[None, :]) % size
    fourier = np.exp(-2j * np.pi * turns / size) / math.sqrt(size)
    axis_kernel = np.exp(-1j * PHASE_COEF * freqs * freqs / (size * size))
    spread = np.conj(fourier) @ (axis_kernel[:, None] * fourier)
    near = spread[:half, :half]
    across = spread[:half, half:]
    even = fourier[0::2, :half]
    odd = fourier[1::2, :half]
    parts = []
    for table in ((near + across) / 2, (near - across) / 2, even, odd, odd.T):
        for value in (table.real, table.imag):
            high = value.astype(jnp.bfloat16)
            parts += [high, (value - high.astype(np.float64)).astype(jnp.bfloat16)]
    return np.stack(parts).reshape(5, 4, half, half)


def cut_own(slot, object_slab, columns, width):
    count = columns.shape[0]
    planes, rows, _ = object_slab.shape

    def body(slot_ref, columns_ref, slab_ref, *refs):
        sems = refs[count]
        copies = []
        for k in range(count):
            start = pl.multiple_of(columns_ref[lax.rem(slot_ref[0] + k, count)], 128)
            copies.append(
                pltpu.make_async_copy(slab_ref.at[:, :, pl.ds(start, width)], refs[k], sems.at[k])
            )
        for copy in copies:
            copy.start()
        for copy in copies:
            copy.wait()

    return pl.pallas_call(
        body,
        out_shape=[on_chip((planes, rows, width))] * count,
        in_specs=[SMEM, SMEM, HBM],
        out_specs=[VMEM] * count,
        scratch_shapes=[pltpu.SemaphoreType.DMA((count,))],
        compiler_params=SMALL,
        name="cut_own",
    )(slot, columns, off_chip(object_slab))


def cut_rims(object_slab, above, below, width):
    count = above.shape[0]
    planes, rows, _ = object_slab.shape

    def body(above_ref, below_ref, slab_ref, for_above, for_below, sems):
        copies = []
        for side, (places_ref, target) in enumerate(((above_ref, for_above), (below_ref, for_below))):
            for k in range(count):
                start = pl.multiple_of(places_ref[k, 1], 128)
                copies.append(
                    pltpu.make_async_copy(
                        slab_ref.at[:, :, pl.ds(start, width)], target.at[k], sems.at[side, k]
                    )
                )
        for copy in copies:
            copy.start()
        for copy in copies:
            copy.wait()

    return pl.pallas_call(
        body,
        out_shape=[on_chip((count, planes, rows, width))] * 2,
        in_specs=[SMEM, SMEM, HBM],
        out_specs=[VMEM] * 2,
        scratch_shapes=[pltpu.SemaphoreType.DMA((2, count))],
        compiler_params=SMALL,
        name="cut_rims",
    )(above, below, off_chip(object_slab))


def blend(places, from_above, from_below):
    count, planes, rows, width = from_above.shape

    def body(places_ref, above_ref, below_ref, out_ref):
        row = lax.broadcasted_iota(jnp.int32, (planes, rows, width), 1)
        for k in range(count):
            out_ref[k] = jnp.where(row < places_ref[k, 0], below_ref[k], above_ref[k])

    return pl.pallas_call(
        body,
        out_shape=on_chip(from_above.shape),
        in_specs=[SMEM, VMEM, VMEM],
        out_specs=VMEM,
        compiler_params=SMALL,
        name="blend",
    )(places, chip(from_above), chip(from_below))


def split(value):
    high = value.astype(jnp.bfloat16)
    return high, (value - high.astype(jnp.float32)).astype(jnp.bfloat16)


def prepare(control, probe, intensity, tables):
    size = probe.shape[-1]
    half = size // 2
    kinds = tables.shape[0]

    def body(control_ref, probe_ref, intensity_ref, tables_ref, left, right, start, sorted_ref, twice, sort_rows, measured, sems):
        slot = control_ref[1]
        shift = pl.multiple_of(control_ref[2], 8)
        fetches = [
            pltpu.make_async_copy(
                intensity_ref.at[slot, :, column * half : (column + 1) * half], measured.at[column], sems.at[column]
            )
            for column in range(2)
        ]
        for fetch in fetches:
            fetch.start()
        twice[:, :size] = probe_ref[...]
        twice[:, size:] = probe_ref[...]
        start[...] = twice[:, pl.ds(shift, size), :]

        @pl.loop(0, kinds)
        def _(kind):
            for place, low in ((0, 0), (1, 1), (2, 0)):
                real = tables_ref[kind, low]
                imag = tables_ref[kind, 2 + low]
                at = size * place
                left[kind, :half, at : at + half] = real
                left[kind, :half, at + half : at + size] = -imag
                left[kind, half:, at : at + half] = imag
                left[kind, half:, at + half : at + size] = real
                right[kind, at : at + half, :half] = real
                right[kind, at : at + half, half:] = imag
                right[kind, at + half : at + size, :half] = -imag
                right[kind, at + half : at + size, half:] = real

        for fetch in fetches:
            fetch.wait()
        source = lax.broadcasted_iota(jnp.int32, (size, size), 0)
        target = lax.broadcasted_iota(jnp.int32, (size, size), 1)
        picked = jnp.where(target < half, 2 * target, 2 * (target - half) + 1)
        sort_rows[...] = (source == picked).astype(jnp.float32).astype(jnp.bfloat16)
        for part in range(2):
            value = jnp.concatenate(
                [measured[column, pl.ds(part, half, stride=2), :] for column in range(2)], axis=1
            )
            total = None
            for _ in range(3):
                high = value.astype(jnp.bfloat16)
                value = value - high.astype(jnp.float32)
                term = jnp.dot(high, sort_rows[...], preferred_element_type=jnp.float32)
                total = term if total is None else total + term
            sorted_ref[part * half : (part + 1) * half] = total

    return pl.pallas_call(
        body,
        out_shape=[
            jax.ShapeDtypeStruct((kinds, size, 3 * size), jnp.bfloat16),
            jax.ShapeDtypeStruct((kinds, 3 * size, size), jnp.bfloat16),
            jax.ShapeDtypeStruct((2, size, size), jnp.float32),
            jax.ShapeDtypeStruct((size, size), jnp.float32),
        ],
        in_specs=[SMEM, VMEM, HBM, VMEM],
        out_specs=[VMEM] * 4,
        scratch_shapes=[
            pltpu.VMEM((2, 2 * size, size), jnp.float32),
            pltpu.VMEM((size, size), jnp.bfloat16),
            pltpu.VMEM((2, size, half), jnp.float32),
            pltpu.SemaphoreType.DMA((2,)),
        ],
        compiler_params=SMALL,
        name="prepare",
    )(control, probe, off_chip(intensity), tables)


def chain(control, owns, halo, left, right, start, measured):
    slices, _, half, size = halo.shape
    low_part = jnp.bfloat16

    def body(*refs):
        control_ref, *own_parts = refs[: slices + 1]
        halo_ref, left_hbm, right_hbm, start_hbm, measured_hbm = refs[slices + 1 : slices + 6]
        grad_parts = refs[slices + 6 : 2 * slices + 6]
        grad_halo, own_ref, grad_own, waves, adjoint, stack, rows, left_ref, right_ref, measured_ref = refs[
            2 * slices + 6 : 2 * slices + 16
        ]
        sems, own_sems, grad_sems = refs[2 * slices + 16 :]
        live = control_ref[0]
        slot = control_ref[1]
        arrivals = [
            pltpu.make_async_copy(
                own_parts[shift], own_ref.at[lax.rem(slot + slices - shift, slices)], own_sems.at[shift]
            )
            for shift in range(slices)
        ]

        def departure(shift):
            return pltpu.make_async_copy(
                grad_own.at[lax.rem(slot + shift, slices)], grad_parts[shift], grad_sems.at[shift]
            )

        near = pl.ds(0, 2)
        rest = pl.ds(2, left_hbm.shape[0] - 2)
        first = [
            pltpu.make_async_copy(start_hbm, waves.at[0], sems.at[0]),
            pltpu.make_async_copy(left_hbm.at[near], left_ref.at[near], sems.at[1]),
            pltpu.make_async_copy(right_hbm.at[near], right_ref.at[near], sems.at[2]),
        ]
        later = [
            pltpu.make_async_copy(left_hbm.at[rest], left_ref.at[rest], sems.at[3]),
            pltpu.make_async_copy(right_hbm.at[rest], right_ref.at[rest], sems.at[4]),
            pltpu.make_async_copy(measured_hbm, measured_ref, sems.at[5]),
        ]

        @pl.when(live == 0)
        def _():
            grad_own[...] = jnp.zeros_like(grad_own)
            grad_halo[...] = jnp.zeros_like(grad_halo)
            for shift in range(slices):
                departure(shift).start()

        def put_stack(branch, part, value):
            high, low = split(value)
            at = part * half
            stack[branch, at : at + half] = high
            stack[branch, size + at : size + at + half] = high
            stack[branch, 2 * size + at : 2 * size + at + half] = low

        def put_rows(branch, block, part, value):
            high, low = split(value)
            at = part * half
            here = slice(block * half, (block + 1) * half)
            rows[branch, here, at : at + half] = high
            rows[branch, here, size + at : size + at + half] = high
            rows[branch, here, 2 * size + at : 2 * size + at + half] = low

        def sandwich(left_kinds, right_kinds, mix):
            for block in range(2):
                middle = jnp.dot(
                    left_ref[left_kinds[block]], stack[block], preferred_element_type=jnp.float32
                )
                for part in range(2):
                    one = middle[part * half : (part + 1) * half, :half]
                    two = middle[part * half : (part + 1) * half, half:]
                    put_rows(0, block, part, one + two if mix else one)
                    put_rows(1, block, part, one - two if mix else two)
            return [
                jnp.dot(rows[branch], right_ref[right_kinds[branch]], preferred_element_type=jnp.float32)
                for branch in range(2)
            ]

        def unmix(first, second, put):
            for column, side in ((0, first + second), (1, first - second)):
                for part in range(2):
                    one = side[:half, part * half : (part + 1) * half]
                    two = side[half:, part * half : (part + 1) * half]
                    put(part, 0, column, one + two)
                    put(part, 1, column, one - two)

        def modulate(index, source, at):
            values = []
            for ref, base in ((own_ref, 0), (halo_ref, half)):
                t_real = 1.0 + ref[index, 0]
                t_imag = ref[index, 1]
                v_real = source[at, 0, base : base + half]
                v_imag = source[at, 1, base : base + half]
                values.append((t_real * v_real - t_imag * v_imag, t_real * v_imag + t_imag * v_real))
            (top_real, top_imag), (low_real, low_imag) = values
            put_stack(0, 0, top_real + low_real)
            put_stack(0, 1, top_imag + low_imag)
            put_stack(1, 0, top_real - low_real)
            put_stack(1, 1, top_imag - low_imag)

        def keep(target, at):
            def put(part, row, column, value):
                target[at, part, row * half : (row + 1) * half, column * half : (column + 1) * half] = value

            return put

        def emit(index):
            for base, target in ((0, grad_own), (half, grad_halo)):
                w_real = waves[index, 0, base : base + half]
                w_imag = waves[index, 1, base : base + half]
                a_real = adjoint[0, 0, base : base + half]
                a_imag = adjoint[0, 1, base : base + half]
                target[index, 0] = w_real * a_real - w_imag * a_imag
                target[index, 1] = -(w_real * a_imag + w_imag * a_real)
            for shift in range(slices):

                @pl.when(lax.rem(slot + shift, slices) == index)
                def _():
                    departure(shift).start()

        @pl.when(live != 0)
        def _():
            for copy in arrivals + first + later:
                copy.start()
            for copy in arrivals + first:
                copy.wait()

            @pl.loop(0, slices - 1)
            def _(index):
                modulate(index, waves, index)
                unmix(*sandwich((0, 1), (0, 1), True), keep(waves, index + 1))

            modulate(slices - 1, waves, slices - 1)
            for copy in later:
                copy.wait()
            for column, far in enumerate(sandwich((2, 3), (2, 4), True)):
                across = slice(column * half, (column + 1) * half)
                for block in range(2):
                    here = slice(block * half, (block + 1) * half)
                    far_real = far[here, :half]
                    far_imag = far[here, half:]
                    misfit = far_real * far_real + far_imag * far_imag - measured_ref[here, across]
                    for part, value in ((0, misfit * far_real), (1, -misfit * far_imag)):
                        high, low = split(value)
                        at = part * half
                        stack[block, at : at + half, across] = high
                        stack[block, size + at : size + at + half, across] = high
                        stack[block, 2 * size + at : 2 * size + at + half, across] = low
            unmix(*sandwich((2, 4), (2, 3), False), keep(adjoint, 0))
            emit(slices - 1)

            @pl.loop(0, slices - 1)
            def _(step):
                index = slices - 1 - step
                modulate(index, adjoint, 0)
                unmix(*sandwich((0, 1), (0, 1), True), keep(adjoint, 0))
                emit(index - 1)

        for shift in range(slices):
            departure(shift).wait()

    return pl.pallas_call(
        body,
        out_shape=[jax.ShapeDtypeStruct(halo.shape[1:], jnp.float32)] * slices + [on_chip(halo.shape)],
        in_specs=[SMEM] + [HBM] * slices + [VMEM] + [HBM] * 4,
        out_specs=[HBM] * slices + [VMEM],
        scratch_shapes=[
            pltpu.VMEM(halo.shape, jnp.float32),
            pltpu.VMEM(halo.shape, jnp.float32),
            pltpu.VMEM((slices, 2, size, size), jnp.float32),
            pltpu.VMEM((1, 2, size, size), jnp.float32),
            pltpu.VMEM((2, 3 * size, size), low_part),
            pltpu.VMEM((2, size, 3 * size), low_part),
            pltpu.VMEM(left.shape, low_part),
            pltpu.VMEM(right.shape, low_part),
            pltpu.VMEM(measured.shape, jnp.float32),
            pltpu.SemaphoreType.DMA((6,)),
            pltpu.SemaphoreType.DMA((slices,)),
            pltpu.SemaphoreType.DMA((slices,)),
        ],
        compiler_params=SMALL,
        name="chain",
    )(
        control,
        *[off_chip(value) for value in owns],
        chip(halo),
        *[off_chip(value) for value in (left, right, start, measured)],
    )


def gather_strip(slot, places, owns, from_above, from_below, width):
    count, planes, strip, size = from_above.shape
    block = 16
    steps = strip // block

    def body(*refs):
        slot_ref, places_ref = refs[:2]
        own_parts = refs[2 : count + 2]
        above_ref, below_ref, out_ref, total, sems = refs[count + 2 :]
        row = lax.broadcasted_iota(jnp.int32, (planes, block, size), 1)

        def copy(step):
            return pltpu.make_async_copy(
                total.at[step % 2], out_ref.at[:, pl.ds(step * block, block)], sems.at[step % 2]
            )

        for step in range(steps):
            here = total.at[step % 2]
            if step >= 2:
                copy(step - 2).wait()
            here[...] = jnp.zeros_like(here)
            across = slice(step * block, (step + 1) * block)
            for group, ref in enumerate((None, above_ref, below_ref)):
                for k in range(count):
                    if group == 0:
                        place = lax.rem(slot_ref[0] + count - k, count)
                        value = own_parts[k][:, across]
                    else:
                        place = k
                        value = ref[k, :, across]
                    start = pl.multiple_of(places_ref[group, place, 1], 128)
                    edge = places_ref[group, place, 0] - step * block
                    if group == 1:
                        value = jnp.where(row < edge, value, 0.0)
                    if group == 2:
                        value = jnp.where(row >= edge, value, 0.0)
                    at = (slice(None), slice(None), pl.ds(start, size))
                    here[at] = here[at] + value
            copy(step).start()
        copy(steps - 2).wait()
        copy(steps - 1).wait()

    return pl.pallas_call(
        body,
        out_shape=jax.ShapeDtypeStruct((planes, strip, width), jnp.float32),
        in_specs=[SMEM, SMEM] + [VMEM] * (count + 2),
        out_specs=HBM,
        scratch_shapes=[
            pltpu.VMEM((2, planes, block, width), jnp.float32),
            pltpu.SemaphoreType.DMA((2,)),
        ],
        compiler_params=SMALL,
        name="gather_strip",
    )(slot, places, *[chip(value) for value in owns], chip(from_above), chip(from_below))


def shifted(values):
    count = len(values)
    return [
        lax.ppermute(value, "cuts", [(i, (i + k) % count) for i in range(count)]) if k else value
        for k, value in enumerate(values)
    ]


def strip_gradient(object_contrast, probe, intensity, positions, counts):
    object_slab = object_contrast[:, 0]
    strip = object_slab.shape[1]
    width = object_slab.shape[2]
    size = probe.shape[-1]
    owner = lax.axis_index("lat")
    slot = lax.axis_index("cuts")
    owners = lax.axis_size("lat")
    downward = [(i, i + 1) for i in range(owners - 1)]
    upward = [(i + 1, i) for i in range(owners - 1)]
    tables = jnp.asarray(wave_tables(size))

    edges = positions[:, 0] - (owner - 1) * strip
    places = jnp.stack([edges, positions[:, 1]], axis=1)
    live = (slot < counts[0]).astype(jnp.int32)
    control = jnp.stack([live, slot, strip - edges[slot]])
    left, right, start, measured = prepare(control, probe, intensity, tables)

    places_above = lax.ppermute(places, "lat", downward)
    places_below = lax.ppermute(places, "lat", upward)
    owns = cut_own(slot[None], object_slab, positions[:, 1], size)
    for_above, for_below = cut_rims(object_slab, places_above, places_below, size)
    from_below = lax.ppermute(for_above, "lat", upward)
    from_above = lax.ppermute(for_below, "lat", downward)
    owns = shifted(owns)
    halo = blend(places, from_above, from_below)
    halo = lax.all_to_all(halo, "cuts", 0, 0, tiled=True)

    *grad_owns, grad_halo = chain(control, owns, halo, left, right, start, measured)

    grad_halo = lax.all_to_all(grad_halo, "cuts", 0, 0, tiled=True)
    back_above = lax.ppermute(grad_halo, "lat", downward)
    back_below = lax.ppermute(grad_halo, "lat", upward)
    grad_owns, grad_halo = lax.optimization_barrier((grad_owns, grad_halo))
    grad_owns = shifted(grad_owns)
    summed = gather_strip(
        slot[None], jnp.stack([places, places_above, places_below]), grad_owns, back_above, back_below, width
    )
    return summed[:, None]


def solution(mesh):
    return jax.shard_map(
        strip_gradient,
        mesh=mesh,
        in_specs=(
            P(None, "cuts", "lat", None),
            P(),
            P("lat", None, None),
            P("lat", None),
            P("lat"),
        ),
        out_specs=P(None, "cuts", "lat", None),
        check_vma=False,
    )
```

profile of v0, /device:TPU:8, one launch (start us, length us, event | category | flops | bytes accessed | tf_op | source)
XLA Modules:
  0.0 119.0 jit_solution(10404340110572031019)
XLA Ops:
  0.0 0.8 slice_bitcast_fusion
  0.8 0.1 copy.29
  0.9 0.1 copy.28
  1.0 0.1 pad_add_fusion.1.places_ref
  1.0 7.1 %collective-permute-start.1 = (s32[4,2]{1,0:T(4,128)S(1)}, s32[4,2]{1,0:T(4,128)S(1)}, u32[]{:S(2)}, u32[]{:S(2)}) collective-permute-start(s32[4,2]{1,0:T(4,128)S(1)} %pad_add_fusion.1.places_ref), channel_id=1, source_target_pairs={{1,0},{2,1},{3,2},{4,3},{5,4},{6,5},{7,6},{8,7},{9,8},{10,9},{11,1... | collective-permute-start | bytes 104 | tf_op jit(solution)/shard_map/ppermute | solution.py:477
  8.1 1.9 %collective-permute-start = (s32[4,2]{1,0:T(4,128)S(1)}, s32[4,2]{1,0:T(4,128)S(1)}, u32[]{:S(2)}, u32[]{:S(2)}) collective-permute-start(s32[4,2]{1,0:T(4,128)S(1)} %pad_add_fusion.1.places_ref), channel_id=1, source_target_pairs={{0,1},{1,2},{2,3},{3,4},{4,5},{5,6},{6,7},{7,8},{8,9},{9,10},{10,1... | collective-permute-start | bytes 104 | tf_op jit(solution)/shard_map/ppermute | solution.py:476
  10.0 0.0 collective-permute-done.1.below_ref
  10.1 5.1 %collective-permute-done.above_ref = s32[4,2]{1,0:T(4,128)S(1)} collective-permute-done((s32[4,2]{1,0:T(4,128)S(1)}, s32[4,2]{1,0:T(4,128)S(1)}, u32[]{:S(2)}, u32[]{:S(2)}) %collective-permute-start) | collective-permute-done | bytes 64 | tf_op jit(solution)/shard_map/ppermute | solution.py:476
  15.1 2.4 %cut_rims.1 = (f32[4,2,128,256]{3,2,1,0:T(8,128)S(1)}, f32[4,2,128,256]{3,2,1,0:T(8,128)S(1)}) custom-call(s32[4,2]{1,0:T(4,128)S(1)} %collective-permute-done.above_ref, s32[4,2]{1,0:T(4,128)S(1)} %collective-permute-done.1.below_ref, f32[2,128,4096]{2,1,0:T(8,128)} %bitcast.17), custom_call_target="tpu_custom_call" | custom-call | tf_op jit(solution)/shard_map/cut_rims/pallas_call | solution.py:98
  17.6 1.9 %collective-permute-start.5 = (f32[4,2,128,256]{3,2,1,0:T(8,128)S(1)}, f32[4,2,128,256]{3,2,1,0:T(8,128)S(1)}, u32[]{:S(2)}, u32[]{:S(2)}) collective-permute-start(f32[4,2,128,256]{3,2,1,0:T(8,128)S(1)} %get-tuple-element.28), channel_id=1, source_target_pairs={{0,1},{1,2},{2,3},{3,4},{4,5},{5,6},{6,7},{7,8},{8,9},{9,10},{10,1... | collective-permute-start | bytes 3145736 | tf_op jit(solution)/shard_map/ppermute | solution.py:481
  19.5 0.0 copy-start.2
  19.5 0.0 copy-start.3
  19.5 5.9 %collective-permute-start.6 = (f32[4,2,128,256]{3,2,1,0:T(8,128)S(1)}, f32[4,2,128,256]{3,2,1,0:T(8,128)S(1)}, u32[]{:S(2)}, u32[]{:S(2)}) collective-permute-start(f32[4,2,128,256]{3,2,1,0:T(8,128)S(1)} %get-tuple-element.29), channel_id=1, source_target_pairs={{1,0},{2,1},{3,2},{4,3},{5,4},{6,5},{7,6},{8,7},{9,8},{10,9},{11,1... | collective-permute-start | bytes 3145736 | tf_op jit(solution)/shard_map/ppermute | solution.py:480
  25.4 10.4 %collective-permute-done.5.above_ref = f32[4,2,128,256]{3,2,1,0:T(8,128)S(1)} collective-permute-done((f32[4,2,128,256]{3,2,1,0:T(8,128)S(1)}, f32[4,2,128,256]{3,2,1,0:T(8,128)S(1)}, u32[]{:S(2)}, u32[]{:S(2)}) %collective-permute-start.5) | collective-permute-done | bytes 1048608 | tf_op jit(solution)/shard_map/ppermute | solution.py:481
  35.8 1.9 %collective-permute-done.6.below_ref = f32[4,2,128,256]{3,2,1,0:T(8,128)S(1)} collective-permute-done((f32[4,2,128,256]{3,2,1,0:T(8,128)S(1)}, f32[4,2,128,256]{3,2,1,0:T(8,128)S(1)}, u32[]{:S(2)}, u32[]{:S(2)}) %collective-permute-start.6) | collective-permute-done | bytes 1048608 | tf_op jit(solution)/shard_map/ppermute | solution.py:480
  37.7 1.6 %blend.1 = f32[4,2,128,256]{3,2,1,0:T(8,128)} custom-call(s32[4,2]{1,0:T(4,128)S(1)} %pad_add_fusion.1.places_ref, f32[4,2,128,256]{3,2,1,0:T(8,128)S(1)} %collective-permute-done.5.above_ref, f32[4,2,128,256]{3,2,1,0:T(8,128)S(1)} %collective-permute-done.6.below_ref), custom_call_target="tpu_custom_call" | custom-call | tf_op jit(solution)/shard_map/blend/pallas_call | solution.py:117
  39.4 4.3 %all-to-all-start = ((f32[4,2,128,256]{3,2,1,0:T(8,128)}), f32[4,2,128,256]{3,2,1,0:T(8,128)S(1)}, u32[]{:S(2)}, u32[]{:S(2)}) async-start(f32[4,2,128,256]{3,2,1,0:T(8,128)} %blend.1), calls=%async_computation | async-start | bytes 2097152 | tf_op jit(solution)/shard_map/all_to_all | solution.py:484
  43.6 1.8 %cut_own.1 = (f32[2,128,256]{2,1,0:T(8,128)S(1)}, f32[2,128,256]{2,1,0:T(8,128)S(1)}, f32[2,128,256]{2,1,0:T(8,128)S(1)}, f32[2,128,256]{2,1,0:T(8,128)S(1)}) custom-call(s32[1]{0:T(128)} %bitcast.slot_ref.refs_0_, s32[4]{0:T(128)S(1)} %get-tuple-element.43.columns_ref, f32[2,128,4096]{2,1,0:T(8,128)} %bitcast.18), custom_call_target="tpu_custom_call" | custom-call | tf_op jit(solution)/shard_map/cut_own/pallas_call | solution.py:68
  45.5 0.7 copy-done.5
  46.2 2.0 %collective-permute-start.2 = (f32[2,128,256]{2,1,0:T(8,128)S(1)}, f32[2,128,256]{2,1,0:T(8,128)S(1)}, u32[]{:S(2)}, u32[]{:S(2)}) collective-permute-start(f32[2,128,256]{2,1,0:T(8,128)S(1)} %get-tuple-element.25), channel_id=1, source_target_pairs={{0,64},{64,128},{128,192},{192,0},{1,65},{65,129},{129,193},{193,1... | collective-permute-start | bytes 786440 | tf_op jit(solution)/shard_map/ppermute | solution.py:453
  48.2 2.7 %collective-permute-start.3 = (f32[2,128,256]{2,1,0:T(8,128)S(1)}, f32[2,128,256]{2,1,0:T(8,128)S(1)}, u32[]{:S(2)}, u32[]{:S(2)}) collective-permute-start(f32[2,128,256]{2,1,0:T(8,128)S(1)} %get-tuple-element.26), channel_id=1, source_target_pairs={{0,128},{64,192},{128,0},{192,64},{1,129},{65,193},{129,1},{193,65... | collective-permute-start | bytes 786440 | tf_op jit(solution)/shard_map/ppermute | solution.py:453
  50.9 1.4 %collective-permute-start.4 = (f32[2,128,256]{2,1,0:T(8,128)S(1)}, f32[2,128,256]{2,1,0:T(8,128)}, u32[]{:S(2)}, u32[]{:S(2)}) collective-permute-start(f32[2,128,256]{2,1,0:T(8,128)S(1)} %get-tuple-element.27), channel_id=1, source_target_pairs={{0,192},{64,0},{128,64},{192,128},{1,193},{65,1},{129,65},{193,129... | collective-permute-start | bytes 786440 | tf_op jit(solution)/shard_map/ppermute | solution.py:453
  53.0 0.5 fusion
  53.5 0.7 pad_add_fusion.2.control_ref.refs_0_
  54.2 1.8 %prepare.1 = (bf16[5,256,768]{2,1,0:T(8,128)(2,1)S(1)}, bf16[5,768,256]{2,1,0:T(8,128)(2,1)S(1)}, f32[2,256,256]{2,1,0:T(8,128)S(1)}, f32[256,256]{1,0:T(8,128)S(1)}) custom-call(s32[3]{0:T(128)S(1)} %pad_add_fusion.2.control_ref.refs_0_, f32[2,256,256]{2,1,0:T(8,128)S(1)} %copy-done.3, f32[4,256,256]{2,1,0:T(8,128)} %intensity_ref.1, ...), custom_call_target="tpu_custom_call" | custom-call | tf_op jit(solution)/shard_map/prepare/pallas_call | solution.py:185
  56.1 0.0 copy-start
  56.1 1.3 %copy-done = bf16[5,256,768]{2,1,0:T(8,128)(2,1)} copy-done((bf16[5,256,768]{2,1,0:T(8,128)(2,1)}, bf16[5,256,768]{2,1,0:T(8,128)(2,1)S(1)}, u32[]{:S(2)}) %copy-start) | copy-done | bytes 1966104
  57.3 1.3 %copy-done.1 = bf16[5,768,256]{2,1,0:T(8,128)(2,1)} copy-done((bf16[5,768,256]{2,1,0:T(8,128)(2,1)}, bf16[5,768,256]{2,1,0:T(8,128)(2,1)S(1)}, u32[]{:S(2)}) %copy-start.1) | copy-done | bytes 1966104
  58.6 0.8 copy-done.4
  59.4 0.7 copy-done.6
  60.1 1.2 collective-permute-done.2.refs_2_
  61.3 3.2 %collective-permute-done.3.refs_3_ = f32[2,128,256]{2,1,0:T(8,128)S(1)} collective-permute-done((f32[2,128,256]{2,1,0:T(8,128)S(1)}, f32[2,128,256]{2,1,0:T(8,128)S(1)}, u32[]{:S(2)}, u32[]{:S(2)}) %collective-permute-start.3) | collective-permute-done | bytes 262176 | tf_op jit(solution)/shard_map/ppermute | solution.py:453
  64.5 0.0 collective-permute-done.4.refs_4_
  64.5 0.0 all-to-all-done.refs_5_
  64.5 0.7 copy-done.8
  65.2 10.4 %chain.1 = (f32[2,128,256]{2,1,0:T(8,128)S(1)}, f32[2,128,256]{2,1,0:T(8,128)S(1)}, f32[2,128,256]{2,1,0:T(8,128)S(1)}, f32[2,128,256]{2,1,0:T(8,128)S(1)}, f32[4,2,128,256]{3,2,1,0:T(8,128)S(1)}) custom-call(s32[3]{0:T(128)S(1)} %pad_add_fusion.2.control_ref.refs_0_, f32[2,128,256]{2,1,0:T(8,128)} %copy-done.5, f32[2,128,256]{2,1,0:T(8,128)} %copy-done.7, ...), custom_call_target="tpu_custom_call" | custom-call | tf_op jit(solution)/shard_map/chain/pallas_call | solution.py:365
  75.6 13.3 %all_to_all.10 = f32[4,2,128,256]{3,2,1,0:T(8,128)S(1)} all-to-all(f32[4,2,128,256]{3,2,1,0:T(8,128)S(1)} %get-tuple-element.38), channel_id=1, replica_groups=mesh['cuts'=4,'lat'=64] {'cuts'}, dimensions={0} | all-to-all | bytes 2097152 | tf_op jit(solution)/shard_map/all_to_all | solution.py:488
  88.9 7.5 %collective-permute-start.11 = (f32[4,2,128,256]{3,2,1,0:T(8,128)S(1)}, f32[4,2,128,256]{3,2,1,0:T(8,128)S(1)}, u32[]{:S(2)}, u32[]{:S(2)}) collective-permute-start(f32[4,2,128,256]{3,2,1,0:T(8,128)S(1)} %all_to_all.10), channel_id=1, source_target_pairs={{1,0},{2,1},{3,2},{4,3},{5,4},{6,5},{7,6},{8,7},{9,8},{10,9},{11,1... | collective-permute-start | bytes 3145736 | tf_op jit(solution)/shard_map/ppermute | solution.py:490
  96.3 1.9 %collective-permute-start.10 = (f32[4,2,128,256]{3,2,1,0:T(8,128)S(1)}, f32[4,2,128,256]{3,2,1,0:T(8,128)S(1)}, u32[]{:S(2)}, u32[]{:S(2)}) collective-permute-start(f32[4,2,128,256]{3,2,1,0:T(8,128)S(1)} %all_to_all.10), channel_id=1, source_target_pairs={{0,1},{1,2},{2,3},{3,4},{4,5},{5,6},{6,7},{7,8},{8,9},{9,10},{10,1... | collective-permute-start | bytes 3145736 | tf_op jit(solution)/shard_map/ppermute | solution.py:489
  98.3 0.6 collective-permute-start.7
  98.9 2.1 %collective-permute-start.8 = (f32[2,128,256]{2,1,0:T(8,128)S(1)}, f32[2,128,256]{2,1,0:T(8,128)S(1)}, u32[]{:S(2)}, u32[]{:S(2)}) collective-permute-start(f32[2,128,256]{2,1,0:T(8,128)S(1)} %get-tuple-element.41), channel_id=1, source_target_pairs={{0,128},{64,192},{128,0},{192,64},{1,129},{65,193},{129,1},{193,65... | collective-permute-start | bytes 786440 | tf_op jit(solution)/shard_map/ppermute | solution.py:453
  101.0 0.8 collective-permute-start.9
  101.8 0.1 fusion.1
  101.9 10.7 %collective-permute-done.7.refs_3_ = f32[2,128,256]{2,1,0:T(8,128)S(1)} collective-permute-done((f32[2,128,256]{2,1,0:T(8,128)S(1)}, f32[2,128,256]{2,1,0:T(8,128)S(1)}, u32[]{:S(2)}, u32[]{:S(2)}) %collective-permute-start.7) | collective-permute-done | bytes 262176 | tf_op jit(solution)/shard_map/ppermute | solution.py:453
  112.5 0.6 collective-permute-done.9.refs_5_
  113.2 0.0 collective-permute-done.11.refs_7_
  113.2 1.4 %collective-permute-done.10.refs_6_ = f32[4,2,128,256]{3,2,1,0:T(8,128)S(1)} collective-permute-done((f32[4,2,128,256]{3,2,1,0:T(8,128)S(1)}, f32[4,2,128,256]{3,2,1,0:T(8,128)S(1)}, u32[]{:S(2)}, u32[]{:S(2)}) %collective-permute-start.10) | collective-permute-done | bytes 1048608 | tf_op jit(solution)/shard_map/ppermute | solution.py:489
  114.6 4.4 %gather_strip.1 = f32[2,128,4096]{2,1,0:T(8,128)} custom-call(s32[1]{0:T(128)} %bitcast.slot_ref.refs_0_, s32[3,4,2]{2,1,0:T(4,128)S(1)} %pad_add_fusion.refs_1_, f32[2,128,256]{2,1,0:T(8,128)S(1)} %get-tuple-element.39.refs_2_, f32[2,128,256]{2,1,0:T(8,128)S(1)} %collective-permute-done.7.refs_3_, f32[2,128,256]{2,1,0:T(8,128)S(1)} %collective-permute-done.8.refs_4_, ...), custom_call_target="tpu_custom_call" | custom-call | tf_op jit(solution)/shard_map/gather_strip/pallas_call | solution.py:436
  (16 shorter events, 0.0 us)
Async XLA Ops:
  1.0 52.0 %copy-start.9 = (s32[4,1]{1,0:T(4,128)}, s32[4,1]{1,0:T(4,128)S(1)}, u32[]{:S(2)}) copy-start(s32[4,1]{1,0:T(4,128)S(1)} %broadcast_subtract_fusion) | copy-start | bytes 52
  1.0 9.0 %collective-permute-start.1 = (s32[4,2]{1,0:T(4,128)S(1)}, s32[4,2]{1,0:T(4,128)S(1)}, u32[]{:S(2)}, u32[]{:S(2)}) collective-permute-start(s32[4,2]{1,0:T(4,128)S(1)} %pad_add_fusion.1.places_ref), channel_id=1, source_target_pairs={{1,0},{2,1},{3,2},{4,3},{5,4},{6,5},{7,6},{8,7},{9,8},{10,9},{11,1... | collective-permute-start | bytes 104 | tf_op jit(solution)/shard_map/ppermute | solution.py:477
  8.1 7.0 %collective-permute-start = (s32[4,2]{1,0:T(4,128)S(1)}, s32[4,2]{1,0:T(4,128)S(1)}, u32[]{:S(2)}, u32[]{:S(2)}) collective-permute-start(s32[4,2]{1,0:T(4,128)S(1)} %pad_add_fusion.1.places_ref), channel_id=1, source_target_pairs={{0,1},{1,2},{2,3},{3,4},{4,5},{5,6},{6,7},{7,8},{8,9},{9,10},{10,1... | collective-permute-start | bytes 104 | tf_op jit(solution)/shard_map/ppermute | solution.py:476
  17.6 18.2 %collective-permute-start.5 = (f32[4,2,128,256]{3,2,1,0:T(8,128)S(1)}, f32[4,2,128,256]{3,2,1,0:T(8,128)S(1)}, u32[]{:S(2)}, u32[]{:S(2)}) collective-permute-start(f32[4,2,128,256]{3,2,1,0:T(8,128)S(1)} %get-tuple-element.28), channel_id=1, source_target_pairs={{0,1},{1,2},{2,3},{3,4},{4,5},{5,6},{6,7},{7,8},{8,9},{9,10},{10,1... | collective-permute-start | bytes 3145736 | tf_op jit(solution)/shard_map/ppermute | solution.py:481
  19.5 34.8 %copy-start.2 = (bf16[5,4,128,128]{3,2,1,0:T(8,128)(2,1)S(1)}, bf16[5,4,128,128]{3,2,1,0:T(8,128)(2,1)}, u32[]{:S(2)}) copy-start(bf16[5,4,128,128]{3,2,1,0:T(8,128)(2,1)} %constant.24.clone.tables_ref) | copy-start | bytes 1966084
  19.5 34.7 %copy-start.3 = (f32[2,256,256]{2,1,0:T(8,128)S(1)}, f32[2,256,256]{2,1,0:T(8,128)}, u32[]{:S(2)}) copy-start(f32[2,256,256]{2,1,0:T(8,128)} %probe_ref.1) | copy-start | bytes 1572868
  19.5 18.2 %collective-permute-start.6 = (f32[4,2,128,256]{3,2,1,0:T(8,128)S(1)}, f32[4,2,128,256]{3,2,1,0:T(8,128)S(1)}, u32[]{:S(2)}, u32[]{:S(2)}) collective-permute-start(f32[4,2,128,256]{3,2,1,0:T(8,128)S(1)} %get-tuple-element.29), channel_id=1, source_target_pairs={{1,0},{2,1},{3,2},{4,3},{5,4},{6,5},{7,6},{8,7},{9,8},{10,9},{11,1... | collective-permute-start | bytes 3145736 | tf_op jit(solution)/shard_map/ppermute | solution.py:480
  39.4 25.1 %all-to-all-start = ((f32[4,2,128,256]{3,2,1,0:T(8,128)}), f32[4,2,128,256]{3,2,1,0:T(8,128)S(1)}, u32[]{:S(2)}, u32[]{:S(2)}) async-start(f32[4,2,128,256]{3,2,1,0:T(8,128)} %blend.1), calls=%async_computation | async-start | bytes 2097152 | tf_op jit(solution)/shard_map/all_to_all | solution.py:484
  45.5 0.7 copy-start.5
  46.2 15.1 %collective-permute-start.2 = (f32[2,128,256]{2,1,0:T(8,128)S(1)}, f32[2,128,256]{2,1,0:T(8,128)S(1)}, u32[]{:S(2)}, u32[]{:S(2)}) collective-permute-start(f32[2,128,256]{2,1,0:T(8,128)S(1)} %get-tuple-element.25), channel_id=1, source_target_pairs={{0,64},{64,128},{128,192},{192,0},{1,65},{65,129},{129,193},{193,1... | collective-permute-start | bytes 786440 | tf_op jit(solution)/shard_map/ppermute | solution.py:453
  48.2 16.3 %collective-permute-start.3 = (f32[2,128,256]{2,1,0:T(8,128)S(1)}, f32[2,128,256]{2,1,0:T(8,128)S(1)}, u32[]{:S(2)}, u32[]{:S(2)}) collective-permute-start(f32[2,128,256]{2,1,0:T(8,128)S(1)} %get-tuple-element.26), channel_id=1, source_target_pairs={{0,128},{64,192},{128,0},{192,64},{1,129},{65,193},{129,1},{193,65... | collective-permute-start | bytes 786440 | tf_op jit(solution)/shard_map/ppermute | solution.py:453
  50.9 13.6 %collective-permute-start.4 = (f32[2,128,256]{2,1,0:T(8,128)S(1)}, f32[2,128,256]{2,1,0:T(8,128)}, u32[]{:S(2)}, u32[]{:S(2)}) collective-permute-start(f32[2,128,256]{2,1,0:T(8,128)S(1)} %get-tuple-element.27), channel_id=1, source_target_pairs={{0,192},{64,0},{128,64},{192,128},{1,193},{65,1},{129,65},{193,129... | collective-permute-start | bytes 786440 | tf_op jit(solution)/shard_map/ppermute | solution.py:453
  56.1 1.3 %copy-start = (bf16[5,256,768]{2,1,0:T(8,128)(2,1)}, bf16[5,256,768]{2,1,0:T(8,128)(2,1)S(1)}, u32[]{:S(2)}) copy-start(bf16[5,256,768]{2,1,0:T(8,128)(2,1)S(1)} %get-tuple-element.30.refs_6_) | copy-start | bytes 5898244
  57.3 1.3 %copy-start.1 = (bf16[5,768,256]{2,1,0:T(8,128)(2,1)}, bf16[5,768,256]{2,1,0:T(8,128)(2,1)S(1)}, u32[]{:S(2)}) copy-start(bf16[5,768,256]{2,1,0:T(8,128)(2,1)S(1)} %get-tuple-element.31.refs_7_) | copy-start | bytes 5898244
  58.6 0.8 copy-start.4
  59.4 0.7 copy-start.6
  61.3 3.2 %copy-start.7 = (f32[2,128,256]{2,1,0:T(8,128)}, f32[2,128,256]{2,1,0:T(8,128)S(1)}, u32[]{:S(2)}) copy-start(f32[2,128,256]{2,1,0:T(8,128)S(1)} %collective-permute-done.2.refs_2_) | copy-start | bytes 786436
  64.5 0.7 copy-start.8
  65.2 36.6 %copy-start.10 = (s32[4,1]{1,0:T(4,128)S(1)}, s32[4,1]{1,0:T(4,128)}, u32[]{:S(2)}) copy-start(s32[4,1]{1,0:T(4,128)} %copy-done.9) | copy-start | bytes 52
  88.9 24.3 %collective-permute-start.11 = (f32[4,2,128,256]{3,2,1,0:T(8,128)S(1)}, f32[4,2,128,256]{3,2,1,0:T(8,128)S(1)}, u32[]{:S(2)}, u32[]{:S(2)}) collective-permute-start(f32[4,2,128,256]{3,2,1,0:T(8,128)S(1)} %all_to_all.10), channel_id=1, source_target_pairs={{1,0},{2,1},{3,2},{4,3},{5,4},{6,5},{7,6},{8,7},{9,8},{10,9},{11,1... | collective-permute-start | bytes 3145736 | tf_op jit(solution)/shard_map/ppermute | solution.py:490
  96.3 18.2 %collective-permute-start.10 = (f32[4,2,128,256]{3,2,1,0:T(8,128)S(1)}, f32[4,2,128,256]{3,2,1,0:T(8,128)S(1)}, u32[]{:S(2)}, u32[]{:S(2)}) collective-permute-start(f32[4,2,128,256]{3,2,1,0:T(8,128)S(1)} %all_to_all.10), channel_id=1, source_target_pairs={{0,1},{1,2},{2,3},{3,4},{4,5},{5,6},{6,7},{7,8},{8,9},{9,10},{10,1... | collective-permute-start | bytes 3145736 | tf_op jit(solution)/shard_map/ppermute | solution.py:489
  98.3 14.3 %collective-permute-start.7 = (f32[2,128,256]{2,1,0:T(8,128)S(1)}, f32[2,128,256]{2,1,0:T(8,128)S(1)}, u32[]{:S(2)}, u32[]{:S(2)}) collective-permute-start(f32[2,128,256]{2,1,0:T(8,128)S(1)} %get-tuple-element.40), channel_id=1, source_target_pairs={{0,64},{64,128},{128,192},{192,0},{1,65},{65,129},{129,193},{193,1... | collective-permute-start | bytes 786440 | tf_op jit(solution)/shard_map/ppermute | solution.py:453
  98.9 13.6 %collective-permute-start.8 = (f32[2,128,256]{2,1,0:T(8,128)S(1)}, f32[2,128,256]{2,1,0:T(8,128)S(1)}, u32[]{:S(2)}, u32[]{:S(2)}) collective-permute-start(f32[2,128,256]{2,1,0:T(8,128)S(1)} %get-tuple-element.41), channel_id=1, source_target_pairs={{0,128},{64,192},{128,0},{192,64},{1,129},{65,193},{129,1},{193,65... | collective-permute-start | bytes 786440 | tf_op jit(solution)/shard_map/ppermute | solution.py:453
  101.0 12.2 %collective-permute-start.9 = (f32[2,128,256]{2,1,0:T(8,128)S(1)}, f32[2,128,256]{2,1,0:T(8,128)S(1)}, u32[]{:S(2)}, u32[]{:S(2)}) collective-permute-start(f32[2,128,256]{2,1,0:T(8,128)S(1)} %get-tuple-element.42), channel_id=1, source_target_pairs={{0,192},{64,0},{128,64},{192,128},{1,193},{65,1},{129,65},{193,129... | collective-permute-start | bytes 786440 | tf_op jit(solution)/shard_map/ppermute | solution.py:453
where the time goes:
time: 119 us
  starting transfers between devices  40.2 us (34%)
  waiting for transfers between devices  34.4 us (29%)
  Pallas kernels  22.5 us (19%)
  blocking collectives  13.3 us (11%)
  local copies, waits for them, and re-layouts  6.4 us (5%)
  other arithmetic  1.4 us (1%)
    ppermute x6, waiting for transfers between devices, shifted(): lax.ppermute(value, 'cuts', [(i, (i + k) % count) for i in range(count)])  15.6 us
    all_to_all x1, blocking collectives, strip_gradient(): grad_halo = lax.all_to_all(grad_halo, 'cuts', 0, 0, tiled=True)  13.3 us
    ppermute x1, waiting for transfers between devices, strip_gradient(): from_above = lax.ppermute(for_below, 'lat', downward)  10.4 us
    pallas_call x1, Pallas kernels, chain(): pl.pallas_call(body, out_shape=[jax.ShapeDtypeStruct(halo.shape[1:], jnp....  10.4 us
    ppermute x6, starting transfers between devices, shifted(): lax.ppermute(value, 'cuts', [(i, (i + k) % count) for i in range(count)])  9.68 us
    ppermute x1, starting transfers between devices, strip_gradient(): back_below = lax.ppermute(grad_halo, 'lat', upward)  7.46 us
    ppermute x1, starting transfers between devices, strip_gradient(): places_below = lax.ppermute(places, 'lat', upward)  7.08 us
    ppermute x1, starting transfers between devices, strip_gradient(): from_below = lax.ppermute(for_above, 'lat', upward)  5.88 us
  transfers between devices with their start and end apart: 13, of which 8 were waited for; matrix products, arithmetic and copies ran while one was open for 1% of the time, Pallas kernels for 3%

commit v1 on v0

--- a/solution.py
+++ b/solution.py
@@ -13,6 +13,7 @@
 VMEM = pl.BlockSpec(memory_space=pltpu.VMEM)
 SMEM = pl.BlockSpec(memory_space=pltpu.SMEM)
 HBM = pl.BlockSpec(memory_space=pltpu.HBM)
+ANY = pl.BlockSpec(memory_space=pl.ANY)
 SMALL = pltpu.CompilerParams(vmem_limit_bytes=16 * 1024 * 1024)
 
 
@@ -185,10 +186,10 @@
     return pl.pallas_call(
         body,
         out_shape=[
-            jax.ShapeDtypeStruct((kinds, size, 3 * size), jnp.bfloat16),
-            jax.ShapeDtypeStruct((kinds, 3 * size, size), jnp.bfloat16),
-            jax.ShapeDtypeStruct((2, size, size), jnp.float32),
-            jax.ShapeDtypeStruct((size, size), jnp.float32),
+            pltpu.HBM((kinds, size, 3 * size), jnp.bfloat16),
+            pltpu.HBM((kinds, 3 * size, size), jnp.bfloat16),
+            pltpu.HBM((2, size, size), jnp.float32),
+            pltpu.HBM((size, size), jnp.float32),
         ],
         in_specs=[SMEM, VMEM, HBM, VMEM],
         out_specs=[VMEM] * 4,
@@ -365,7 +366,7 @@
     return pl.pallas_call(
         body,
         out_shape=[jax.ShapeDtypeStruct(halo.shape[1:], jnp.float32)] * slices + [on_chip(halo.shape)],
-        in_specs=[SMEM] + [HBM] * slices + [VMEM] + [HBM] * 4,
+        in_specs=[SMEM] + [ANY] * slices + [VMEM] + [HBM] * 4,
         out_specs=[HBM] * slices + [VMEM],
         scratch_shapes=[
             pltpu.VMEM(halo.shape, jnp.float32),
@@ -385,66 +386,88 @@
         name="chain",
     )(
         control,
-        *[off_chip(value) for value in owns],
+        *owns,
         chip(halo),
         *[off_chip(value) for value in (left, right, start, measured)],
     )
 
 
-def gather_strip(slot, places, owns, from_above, from_below, width):
+def gather_rims(above, below, from_above, from_below, width):
     count, planes, strip, size = from_above.shape
-    block = 16
+
+    def body(places_above, places_below, above_ref, below_ref, out_ref):
+        row = lax.broadcasted_iota(jnp.int32, (planes, strip, size), 1)
+        out_ref[...] = jnp.zeros_like(out_ref)
+        for places_ref, ref, upper in ((places_above, above_ref, True), (places_below, below_ref, False)):
+            for k in range(count):
+                start = pl.multiple_of(places_ref[k, 1], 128)
+                mask = row < places_ref[k, 0] if upper else row >= places_ref[k, 0]
+                at = (slice(None), slice(None), pl.ds(start, size))
+                out_ref[at] = out_ref[at] + jnp.where(mask, ref[k], 0.0)
+
+    return pl.pallas_call(
+        body,
+        out_shape=on_chip((planes, strip, width)),
+        in_specs=[SMEM, SMEM, VMEM, VMEM],
+        out_specs=VMEM,
+        compiler_params=SMALL,
+        name="gather_rims",
+    )(above, below, chip(from_above), chip(from_below))
+
+
+def gather_strip(slot, places, owns, rims):
+    count = len(owns)
+    _, strip, size = owns[0].shape
+    block = 32
     steps = strip // block
 
-    def body(*refs):
-        slot_ref, places_ref = refs[:2]
-        own_parts = refs[2 : count + 2]
-        above_ref, below_ref, out_ref, total, sems = refs[count + 2 :]
-        row = lax.broadcasted_iota(jnp.int32, (planes, block, size), 1)
+    def body(slot_ref, places_ref, rims_ref, *refs):
+        out_ref, total, sems = refs[count:]
 
         def copy(step):
-            return pltpu.make_async_copy(
-                total.at[step % 2], out_ref.at[:, pl.ds(step * block, block)], sems.at[step % 2]
-            )
+            here = pl.ds(step * block, block)
+            return pltpu.make_async_copy(total.at[:, here], out_ref.at[:, here], sems.at[step])
 
         for step in range(steps):
-            here = total.at[step % 2]
-            if step >= 2:
-                copy(step - 2).wait()
-            here[...] = jnp.zeros_like(here)
             across = slice(step * block, (step + 1) * block)
-            for group, ref in enumerate((None, above_ref, below_ref)):
-                for k in range(count):
-                    if group == 0:
-                        place = lax.rem(slot_ref[0] + count - k, count)
-                        value = own_parts[k][:, across]
-                    else:
-                        place = k
-                        value = ref[k, :, across]
-                    start = pl.multiple_of(places_ref[group, place, 1], 128)
-                    edge = places_ref[group, place, 0] - step * block
-                    if group == 1:
-                        value = jnp.where(row < edge, value, 0.0)
-                    if group == 2:
-                        value = jnp.where(row >= edge, value, 0.0)
-                    at = (slice(None), slice(None), pl.ds(start, size))
-                    here[at] = here[at] + value
+            total[:, across] = rims_ref[:, across]
+            for k in range(count):
+                start = pl.multiple_of(places_ref[lax.rem(slot_ref[0] + count - k, count), 1], 128)
+                at = (slice(None), across, pl.ds(start, size))
+                total[at] = total[at] + refs[k][:, across]
             copy(step).start()
-        copy(steps - 2).wait()
-        copy(steps - 1).wait()
-
-    return pl.pallas_call(
-        body,
-        out_shape=jax.ShapeDtypeStruct((planes, strip, width), jnp.float32),
-        in_specs=[SMEM, SMEM] + [VMEM] * (count + 2),
+        for step in range(steps):
+            copy(step).wait()
+
+    return pl.pallas_call(
+        body,
+        out_shape=jax.ShapeDtypeStruct(rims.shape, jnp.float32),
+        in_specs=[SMEM, SMEM] + [VMEM] * (count + 1),
         out_specs=HBM,
         scratch_shapes=[
-            pltpu.VMEM((2, planes, block, width), jnp.float32),
-            pltpu.SemaphoreType.DMA((2,)),
+            pltpu.VMEM(rims.shape, jnp.float32),
+            pltpu.SemaphoreType.DMA((steps,)),
         ],
         compiler_params=SMALL,
         name="gather_strip",
-    )(slot, places, *[chip(value) for value in owns], chip(from_above), chip(from_below))
+    )(slot, places, chip(rims), *[chip(value) for value in owns])
+
+
+def steering(slot, counts, places, strip):
+    def body(slot_ref, counts_ref, places_ref, out_ref):
+        slot = slot_ref[0]
+        out_ref[0] = (slot < counts_ref[0]).astype(jnp.int32)
+        out_ref[1] = slot
+        out_ref[2] = strip - places_ref[slot, 0]
+
+    return pl.pallas_call(
+        body,
+        out_shape=jax.ShapeDtypeStruct((3,), jnp.int32),
+        in_specs=[SMEM] * 3,
+        out_specs=SMEM,
+        compiler_params=SMALL,
+        name="steering",
+    )(slot, counts, places)
 
 
 def shifted(values):
@@ -469,17 +492,16 @@
 
     edges = positions[:, 0] - (owner - 1) * strip
     places = jnp.stack([edges, positions[:, 1]], axis=1)
-    live = (slot < counts[0]).astype(jnp.int32)
-    control = jnp.stack([live, slot, strip - edges[slot]])
-    left, right, start, measured = prepare(control, probe, intensity, tables)
-
+    slot = slot[None]
     places_above = lax.ppermute(places, "lat", downward)
     places_below = lax.ppermute(places, "lat", upward)
-    owns = cut_own(slot[None], object_slab, positions[:, 1], size)
+    owns = cut_own(slot, object_slab, positions[:, 1], size)
     for_above, for_below = cut_rims(object_slab, places_above, places_below, size)
     from_below = lax.ppermute(for_above, "lat", upward)
     from_above = lax.ppermute(for_below, "lat", downward)
     owns = shifted(owns)
+    control = steering(slot, counts, places, strip)
+    left, right, start, measured = prepare(control, probe, intensity, tables)
     halo = blend(places, from_above, from_below)
     halo = lax.all_to_all(halo, "cuts", 0, 0, tiled=True)
 
@@ -490,9 +512,8 @@
     back_below = lax.ppermute(grad_halo, "lat", upward)
     grad_owns, grad_halo = lax.optimization_barrier((grad_owns, grad_halo))
     grad_owns = shifted(grad_owns)
-    summed = gather_strip(
-        slot[None], jnp.stack([places, places_above, places_below]), grad_owns, back_above, back_below, width
-    )
+    rims = gather_rims(places_above, places_below, back_above, back_below, width)
+    summed = gather_strip(slot, places, grad_owns, rims)
     return summed[:, None]
 
 

time: 119 us -> 114 us (0.958)
  the two profiles are of different devices: /device:TPU:8 before, /device:TPU:24 now
where the time goes in v1:
time: 114 us
  starting transfers between devices  37.5 us (33%)
  waiting for transfers between devices  37.5 us (33%)
  Pallas kernels  23.8 us (21%)
  blocking collectives  13.3 us (12%)
    all_to_all x1, blocking collectives, strip_gradient(): grad_halo = lax.all_to_all(grad_halo, 'cuts', 0, 0, tiled=True)  13.3 us
    ppermute x1, waiting for transfers between devices, strip_gradient(): from_above = lax.ppermute(for_below, 'lat', downward)  10.4 us
    ppermute x6, starting transfers between devices, shifted(): lax.ppermute(value, 'cuts', [(i, (i + k) % count) for i in range(count)])  9.77 us
    pallas_call x1, Pallas kernels, chain(): pl.pallas_call(body, out_shape=[jax.ShapeDtypeStruct(halo.shape[1:], jnp....  9.31 us
    ppermute x1, starting transfers between devices, strip_gradient(): places_below = lax.ppermute(places, 'lat', upward)  7.37 us
    ppermute x6, waiting for transfers between devices, shifted(): lax.ppermute(value, 'cuts', [(i, (i + k) % count) for i in range(count)])  7.36 us
    ppermute x1, waiting for transfers between devices, strip_gradient(): back_below = lax.ppermute(grad_halo, 'lat', upward)  6.84 us
    ppermute x1, waiting for transfers between devices, strip_gradient(): back_above = lax.ppermute(grad_halo, 'lat', downward)  5.93 us
  transfers between devices with their start and end apart: 13, of which 7 were waited for; matrix products, arithmetic and copies ran while one was open for 0% of the time, Pallas kernels for 7%

profile of v1, /device:TPU:24, one launch (start us, length us, event | category | flops | bytes accessed | tf_op | source)
XLA Modules:
  0.0 113.9 jit_solution(16443484746311616277)
XLA Ops:
  0.0 0.8 slice_bitcast_fusion
  0.8 0.1 copy.13
  0.9 0.1 copy.14
  0.9 0.1 pad_add_fusion.places_ref
  1.0 7.4 %collective-permute-start.1 = (s32[4,2]{1,0:T(4,128)S(1)}, s32[4,2]{1,0:T(4,128)S(1)}, u32[]{:S(2)}, u32[]{:S(2)}) collective-permute-start(s32[4,2]{1,0:T(4,128)S(1)} %pad_add_fusion.places_ref), channel_id=1, source_target_pairs={{1,0},{2,1},{3,2},{4,3},{5,4},{6,5},{7,6},{8,7},{9,8},{10,9},{11,1... | collective-permute-start | bytes 104 | tf_op jit(solution)/shard_map/ppermute | solution.py:497
  8.4 1.9 %collective-permute-start = (s32[4,2]{1,0:T(4,128)S(1)}, s32[4,2]{1,0:T(4,128)S(1)}, u32[]{:S(2)}, u32[]{:S(2)}) collective-permute-start(s32[4,2]{1,0:T(4,128)S(1)} %pad_add_fusion.places_ref), channel_id=1, source_target_pairs={{0,1},{1,2},{2,3},{3,4},{4,5},{5,6},{6,7},{7,8},{8,9},{9,10},{10,1... | collective-permute-start | bytes 104 | tf_op jit(solution)/shard_map/ppermute | solution.py:496
  10.3 0.0 collective-permute-done.1.below_ref.places_below
  10.3 5.1 %collective-permute-done.above_ref.places_above = s32[4,2]{1,0:T(4,128)S(1)} collective-permute-done((s32[4,2]{1,0:T(4,128)S(1)}, s32[4,2]{1,0:T(4,128)S(1)}, u32[]{:S(2)}, u32[]{:S(2)}) %collective-permute-start) | collective-permute-done | bytes 64 | tf_op jit(solution)/shard_map/ppermute | solution.py:496
  15.4 2.2 %cut_rims.1 = (f32[4,2,128,256]{3,2,1,0:T(8,128)S(1)}, f32[4,2,128,256]{3,2,1,0:T(8,128)S(1)}) custom-call(s32[4,2]{1,0:T(4,128)S(1)} %collective-permute-done.above_ref.places_above, s32[4,2]{1,0:T(4,128)S(1)} %collective-permute-done.1.below_ref.places_below, f32[2,128,4096]{2,1,0:T(8,128)} %bitcast.7), custom_call_target="tpu_custom_call" | custom-call | tf_op jit(solution)/shard_map/cut_rims/pallas_call | solution.py:99
  17.7 1.9 %collective-permute-start.5 = (f32[4,2,128,256]{3,2,1,0:T(8,128)S(1)}, f32[4,2,128,256]{3,2,1,0:T(8,128)S(1)}, u32[]{:S(2)}, u32[]{:S(2)}) collective-permute-start(f32[4,2,128,256]{3,2,1,0:T(8,128)S(1)} %get-tuple-element.28), channel_id=1, source_target_pairs={{0,1},{1,2},{2,3},{3,4},{4,5},{5,6},{6,7},{7,8},{8,9},{9,10},{10,1... | collective-permute-start | bytes 3145736 | tf_op jit(solution)/shard_map/ppermute | solution.py:501
  19.6 0.0 copy-start
  19.6 0.0 copy-start.1
  19.6 5.9 %collective-permute-start.6 = (f32[4,2,128,256]{3,2,1,0:T(8,128)S(1)}, f32[4,2,128,256]{3,2,1,0:T(8,128)S(1)}, u32[]{:S(2)}, u32[]{:S(2)}) collective-permute-start(f32[4,2,128,256]{3,2,1,0:T(8,128)S(1)} %get-tuple-element.29), channel_id=1, source_target_pairs={{1,0},{2,1},{3,2},{4,3},{5,4},{6,5},{7,6},{8,7},{9,8},{10,9},{11,1... | collective-permute-start | bytes 3145736 | tf_op jit(solution)/shard_map/ppermute | solution.py:500
  25.5 10.4 %collective-permute-done.5.above_ref = f32[4,2,128,256]{3,2,1,0:T(8,128)S(1)} collective-permute-done((f32[4,2,128,256]{3,2,1,0:T(8,128)S(1)}, f32[4,2,128,256]{3,2,1,0:T(8,128)S(1)}, u32[]{:S(2)}, u32[]{:S(2)}) %collective-permute-start.5) | collective-permute-done | bytes 1048608 | tf_op jit(solution)/shard_map/ppermute | solution.py:501
  35.9 1.9 %collective-permute-done.6.below_ref = f32[4,2,128,256]{3,2,1,0:T(8,128)S(1)} collective-permute-done((f32[4,2,128,256]{3,2,1,0:T(8,128)S(1)}, f32[4,2,128,256]{3,2,1,0:T(8,128)S(1)}, u32[]{:S(2)}, u32[]{:S(2)}) %collective-permute-start.6) | collective-permute-done | bytes 1048608 | tf_op jit(solution)/shard_map/ppermute | solution.py:500
  37.8 1.6 %blend.1 = f32[4,2,128,256]{3,2,1,0:T(8,128)} custom-call(s32[4,2]{1,0:T(4,128)S(1)} %pad_add_fusion.places_ref, f32[4,2,128,256]{3,2,1,0:T(8,128)S(1)} %collective-permute-done.5.above_ref, f32[4,2,128,256]{3,2,1,0:T(8,128)S(1)} %collective-permute-done.6.below_ref), custom_call_target="tpu_custom_call" | custom-call | tf_op jit(solution)/shard_map/blend/pallas_call | solution.py:118
  39.5 4.3 %all-to-all-start = ((f32[4,2,128,256]{3,2,1,0:T(8,128)}), f32[4,2,128,256]{3,2,1,0:T(8,128)S(1)}, u32[]{:S(2)}, u32[]{:S(2)}) async-start(f32[4,2,128,256]{3,2,1,0:T(8,128)} %blend.1), calls=%async_computation | async-start | bytes 2097152 | tf_op jit(solution)/shard_map/all_to_all | solution.py:506
  43.7 1.8 %cut_own.1 = (f32[2,128,256]{2,1,0:T(8,128)S(1)}, f32[2,128,256]{2,1,0:T(8,128)S(1)}, f32[2,128,256]{2,1,0:T(8,128)S(1)}, f32[2,128,256]{2,1,0:T(8,128)S(1)}) custom-call(s32[1]{0:T(128)} %bitcast.slot_ref, s32[4]{0:T(128)S(1)} %get-tuple-element.43.columns_ref, f32[2,128,4096]{2,1,0:T(8,128)} %bitcast.8), custom_call_target="tpu_custom_call" | custom-call | tf_op jit(solution)/shard_map/cut_own/pallas_call | solution.py:69
  45.5 2.1 %collective-permute-start.2 = (f32[2,128,256]{2,1,0:T(8,128)S(1)}, f32[2,128,256]{2,1,0:T(8,128)S(1)}, u32[]{:S(2)}, u32[]{:S(2)}) collective-permute-start(f32[2,128,256]{2,1,0:T(8,128)S(1)} %get-tuple-element.25), channel_id=1, source_target_pairs={{0,64},{64,128},{128,192},{192,0},{1,65},{65,129},{129,193},{193,1... | collective-permute-start | bytes 786440 | tf_op jit(solution)/shard_map/ppermute | solution.py:476
  47.6 2.7 %collective-permute-start.3 = (f32[2,128,256]{2,1,0:T(8,128)S(1)}, f32[2,128,256]{2,1,0:T(8,128)S(1)}, u32[]{:S(2)}, u32[]{:S(2)}) collective-permute-start(f32[2,128,256]{2,1,0:T(8,128)S(1)} %get-tuple-element.26), channel_id=1, source_target_pairs={{0,128},{64,192},{128,0},{192,64},{1,129},{65,193},{129,1},{193,65... | collective-permute-start | bytes 786440 | tf_op jit(solution)/shard_map/ppermute | solution.py:476
  50.3 1.5 %collective-permute-start.4 = (f32[2,128,256]{2,1,0:T(8,128)S(1)}, f32[2,128,256]{2,1,0:T(8,128)S(1)}, u32[]{:S(2)}, u32[]{:S(2)}) collective-permute-start(f32[2,128,256]{2,1,0:T(8,128)S(1)} %get-tuple-element.27), channel_id=1, source_target_pairs={{0,192},{64,0},{128,64},{192,128},{1,193},{65,1},{129,65},{193,129... | collective-permute-start | bytes 786440 | tf_op jit(solution)/shard_map/ppermute | solution.py:476
  52.4 1.2 %steering.1.control_ref.refs_0_ = s32[3]{0:T(128)S(1)} custom-call(s32[1]{0:T(128)} %bitcast.slot_ref, s32[1]{0:T(128)S(6)} %copy.16.counts_ref, s32[4,2]{1,0:T(4,128)S(1)} %pad_add_fusion.places_ref), custom_call_target="tpu_custom_call" | custom-call | tf_op jit(solution)/shard_map/steering/pallas_call | solution.py:463
  53.6 0.0 copy-done
  53.6 0.0 copy-done.1
  53.6 3.7 %prepare.1 = (bf16[5,256,768]{2,1,0:T(8,128)(2,1)}, bf16[5,768,256]{2,1,0:T(8,128)(2,1)}, f32[2,256,256]{2,1,0:T(8,128)}, f32[256,256]{1,0:T(8,128)}) custom-call(s32[3]{0:T(128)S(1)} %steering.1.control_ref.refs_0_, f32[2,256,256]{2,1,0:T(8,128)S(1)} %copy-done.1, f32[4,256,256]{2,1,0:T(8,128)} %intensity_ref.1, bf16[5,4,128,128]{3,2,1,0:T(8,128)(2,1)S(1)} %copy-done), custom_call_target="tpu_custom_call" | custom-call | tf_op jit(solution)/shard_map/prepare/pallas_call | solution.py:186
  57.3 4.2 %collective-permute-done.2.refs_2_ = f32[2,128,256]{2,1,0:T(8,128)S(1)} collective-permute-done((f32[2,128,256]{2,1,0:T(8,128)S(1)}, f32[2,128,256]{2,1,0:T(8,128)S(1)}, u32[]{:S(2)}, u32[]{:S(2)}) %collective-permute-start.2) | collective-permute-done | bytes 262176 | tf_op jit(solution)/shard_map/ppermute | solution.py:476
  61.5 3.2 %collective-permute-done.3.refs_3_ = f32[2,128,256]{2,1,0:T(8,128)S(1)} collective-permute-done((f32[2,128,256]{2,1,0:T(8,128)S(1)}, f32[2,128,256]{2,1,0:T(8,128)S(1)}, u32[]{:S(2)}, u32[]{:S(2)}) %collective-permute-start.3) | collective-permute-done | bytes 262176 | tf_op jit(solution)/shard_map/ppermute | solution.py:476
  64.7 0.0 collective-permute-done.4.refs_4_
  64.7 0.0 all-to-all-done.refs_5_
  64.7 9.3 %chain.1 = (f32[2,128,256]{2,1,0:T(8,128)S(1)}, f32[2,128,256]{2,1,0:T(8,128)S(1)}, f32[2,128,256]{2,1,0:T(8,128)S(1)}, f32[2,128,256]{2,1,0:T(8,128)S(1)}, f32[4,2,128,256]{3,2,1,0:T(8,128)S(1)}) custom-call(s32[3]{0:T(128)S(1)} %steering.1.control_ref.refs_0_, f32[2,128,256]{2,1,0:T(8,128)S(1)} %get-tuple-element.24.refs_1_, ...), custom_call_target="tpu_custom_call" | custom-call | tf_op jit(solution)/shard_map/chain/pallas_call | solution.py:366
  74.0 13.3 %all_to_all.10 = f32[4,2,128,256]{3,2,1,0:T(8,128)S(1)} all-to-all(f32[4,2,128,256]{3,2,1,0:T(8,128)S(1)} %get-tuple-element.34), channel_id=1, replica_groups=mesh['cuts'=4,'lat'=64] {'cuts'}, dimensions={0} | all-to-all | bytes 2097152 | tf_op jit(solution)/shard_map/all_to_all | solution.py:510
  87.3 4.4 %collective-permute-start.8 = (f32[4,2,128,256]{3,2,1,0:T(8,128)S(1)}, f32[4,2,128,256]{3,2,1,0:T(8,128)S(1)}, u32[]{:S(2)}, u32[]{:S(2)}) collective-permute-start(f32[4,2,128,256]{3,2,1,0:T(8,128)S(1)} %all_to_all.10), channel_id=1, source_target_pairs={{1,0},{2,1},{3,2},{4,3},{5,4},{6,5},{7,6},{8,7},{9,8},{10,9},{11,1... | collective-permute-start | bytes 3145736 | tf_op jit(solution)/shard_map/ppermute | solution.py:512
  91.7 1.9 %collective-permute-start.7 = (f32[4,2,128,256]{3,2,1,0:T(8,128)S(1)}, f32[4,2,128,256]{3,2,1,0:T(8,128)S(1)}, u32[]{:S(2)}, u32[]{:S(2)}) collective-permute-start(f32[4,2,128,256]{3,2,1,0:T(8,128)S(1)} %all_to_all.10), channel_id=1, source_target_pairs={{0,1},{1,2},{2,3},{3,4},{4,5},{5,6},{6,7},{7,8},{8,9},{9,10},{10,1... | collective-permute-start | bytes 3145736 | tf_op jit(solution)/shard_map/ppermute | solution.py:511
  93.6 0.6 collective-permute-start.9
  94.3 2.1 %collective-permute-start.10 = (f32[2,128,256]{2,1,0:T(8,128)S(1)}, f32[2,128,256]{2,1,0:T(8,128)S(1)}, u32[]{:S(2)}, u32[]{:S(2)}) collective-permute-start(f32[2,128,256]{2,1,0:T(8,128)S(1)} %get-tuple-element.41), channel_id=1, source_target_pairs={{0,128},{64,192},{128,0},{192,64},{1,129},{65,193},{129,1},{193,65... | collective-permute-start | bytes 786440 | tf_op jit(solution)/shard_map/ppermute | solution.py:476
  96.4 0.8 collective-permute-start.11
  97.2 6.8 %collective-permute-done.8.below_ref = f32[4,2,128,256]{3,2,1,0:T(8,128)S(1)} collective-permute-done((f32[4,2,128,256]{3,2,1,0:T(8,128)S(1)}, f32[4,2,128,256]{3,2,1,0:T(8,128)S(1)}, u32[]{:S(2)}, u32[]{:S(2)}) %collective-permute-start.8) | collective-permute-done | bytes 1048608 | tf_op jit(solution)/shard_map/ppermute | solution.py:512
  104.0 5.9 %collective-permute-done.7.above_ref = f32[4,2,128,256]{3,2,1,0:T(8,128)S(1)} collective-permute-done((f32[4,2,128,256]{3,2,1,0:T(8,128)S(1)}, f32[4,2,128,256]{3,2,1,0:T(8,128)S(1)}, u32[]{:S(2)}, u32[]{:S(2)}) %collective-permute-start.7) | collective-permute-done | bytes 1048608 | tf_op jit(solution)/shard_map/ppermute | solution.py:511
  109.9 1.2 %gather_rims.1.rims_ref = f32[2,128,4096]{2,1,0:T(8,128)S(1)} custom-call(s32[4,2]{1,0:T(4,128)S(1)} %collective-permute-done.above_ref.places_above, s32[4,2]{1,0:T(4,128)S(1)} %collective-permute-done.1.below_ref.places_below, f32[4,2,128,256]{3,2,1,0:T(8,128)S(1)} %collective-permute-done.7.above_ref, f32[4,2,128,256]{3,2,1,0:T(8,128)S(1)} %collective-permute-done.8.below_ref), custom_call_target="tpu_custom_call" | custom-call | tf_op jit(solution)/shard_map/gather_rims/pallas_call | solution.py:408
  111.1 0.0 collective-permute-done.9.refs_1_
  111.1 0.0 collective-permute-done.10.refs_2_
  111.2 0.0 collective-permute-done.11.refs_3_
  111.2 2.7 %gather_strip.1 = f32[2,128,4096]{2,1,0:T(8,128)} custom-call(s32[1]{0:T(128)} %bitcast.slot_ref, s32[4,2]{1,0:T(4,128)S(1)} %pad_add_fusion.places_ref, f32[2,128,4096]{2,1,0:T(8,128)S(1)} %gather_rims.1.rims_ref, f32[2,128,256]{2,1,0:T(8,128)S(1)} %get-tuple-element.39.refs_0_, f32[2,128,256]{2,1,0:T(8,128)S(1)} %collective-permute-done.9.refs_1_, ...), custom_call_target="tpu_custom_call" | custom-call | tf_op jit(solution)/shard_map/gather_strip/pallas_call | solution.py:442
  (1 shorter events, 0.0 us)
Async XLA Ops:
  1.0 9.3 %collective-permute-start.1 = (s32[4,2]{1,0:T(4,128)S(1)}, s32[4,2]{1,0:T(4,128)S(1)}, u32[]{:S(2)}, u32[]{:S(2)}) collective-permute-start(s32[4,2]{1,0:T(4,128)S(1)} %pad_add_fusion.places_ref), channel_id=1, source_target_pairs={{1,0},{2,1},{3,2},{4,3},{5,4},{6,5},{7,6},{8,7},{9,8},{10,9},{11,1... | collective-permute-start | bytes 104 | tf_op jit(solution)/shard_map/ppermute | solution.py:497
  8.4 7.0 %collective-permute-start = (s32[4,2]{1,0:T(4,128)S(1)}, s32[4,2]{1,0:T(4,128)S(1)}, u32[]{:S(2)}, u32[]{:S(2)}) collective-permute-start(s32[4,2]{1,0:T(4,128)S(1)} %pad_add_fusion.places_ref), channel_id=1, source_target_pairs={{0,1},{1,2},{2,3},{3,4},{4,5},{5,6},{6,7},{7,8},{8,9},{9,10},{10,1... | collective-permute-start | bytes 104 | tf_op jit(solution)/shard_map/ppermute | solution.py:496
  17.7 18.2 %collective-permute-start.5 = (f32[4,2,128,256]{3,2,1,0:T(8,128)S(1)}, f32[4,2,128,256]{3,2,1,0:T(8,128)S(1)}, u32[]{:S(2)}, u32[]{:S(2)}) collective-permute-start(f32[4,2,128,256]{3,2,1,0:T(8,128)S(1)} %get-tuple-element.28), channel_id=1, source_target_pairs={{0,1},{1,2},{2,3},{3,4},{4,5},{5,6},{6,7},{7,8},{8,9},{9,10},{10,1... | collective-permute-start | bytes 3145736 | tf_op jit(solution)/shard_map/ppermute | solution.py:501
  19.6 34.0 %copy-start = (bf16[5,4,128,128]{3,2,1,0:T(8,128)(2,1)S(1)}, bf16[5,4,128,128]{3,2,1,0:T(8,128)(2,1)}, u32[]{:S(2)}) copy-start(bf16[5,4,128,128]{3,2,1,0:T(8,128)(2,1)} %constant.16.clone.tables_ref) | copy-start | bytes 1966084
  19.6 34.0 %copy-start.1 = (f32[2,256,256]{2,1,0:T(8,128)S(1)}, f32[2,256,256]{2,1,0:T(8,128)}, u32[]{:S(2)}) copy-start(f32[2,256,256]{2,1,0:T(8,128)} %probe_ref.1) | copy-start | bytes 1572868
  19.6 18.2 %collective-permute-start.6 = (f32[4,2,128,256]{3,2,1,0:T(8,128)S(1)}, f32[4,2,128,256]{3,2,1,0:T(8,128)S(1)}, u32[]{:S(2)}, u32[]{:S(2)}) collective-permute-start(f32[4,2,128,256]{3,2,1,0:T(8,128)S(1)} %get-tuple-element.29), channel_id=1, source_target_pairs={{1,0},{2,1},{3,2},{4,3},{5,4},{6,5},{7,6},{8,7},{9,8},{10,9},{11,1... | collective-permute-start | bytes 3145736 | tf_op jit(solution)/shard_map/ppermute | solution.py:500
  39.5 25.2 %all-to-all-start = ((f32[4,2,128,256]{3,2,1,0:T(8,128)}), f32[4,2,128,256]{3,2,1,0:T(8,128)S(1)}, u32[]{:S(2)}, u32[]{:S(2)}) async-start(f32[4,2,128,256]{3,2,1,0:T(8,128)} %blend.1), calls=%async_computation | async-start | bytes 2097152 | tf_op jit(solution)/shard_map/all_to_all | solution.py:506
  45.5 16.0 %collective-permute-start.2 = (f32[2,128,256]{2,1,0:T(8,128)S(1)}, f32[2,128,256]{2,1,0:T(8,128)S(1)}, u32[]{:S(2)}, u32[]{:S(2)}) collective-permute-start(f32[2,128,256]{2,1,0:T(8,128)S(1)} %get-tuple-element.25), channel_id=1, source_target_pairs={{0,64},{64,128},{128,192},{192,0},{1,65},{65,129},{129,193},{193,1... | collective-permute-start | bytes 786440 | tf_op jit(solution)/shard_map/ppermute | solution.py:476
  47.6 17.1 %collective-permute-start.3 = (f32[2,128,256]{2,1,0:T(8,128)S(1)}, f32[2,128,256]{2,1,0:T(8,128)S(1)}, u32[]{:S(2)}, u32[]{:S(2)}) collective-permute-start(f32[2,128,256]{2,1,0:T(8,128)S(1)} %get-tuple-element.26), channel_id=1, source_target_pairs={{0,128},{64,192},{128,0},{192,64},{1,129},{65,193},{129,1},{193,65... | collective-permute-start | bytes 786440 | tf_op jit(solution)/shard_map/ppermute | solution.py:476
  50.3 14.4 %collective-permute-start.4 = (f32[2,128,256]{2,1,0:T(8,128)S(1)}, f32[2,128,256]{2,1,0:T(8,128)S(1)}, u32[]{:S(2)}, u32[]{:S(2)}) collective-permute-start(f32[2,128,256]{2,1,0:T(8,128)S(1)} %get-tuple-element.27), channel_id=1, source_target_pairs={{0,192},{64,0},{128,64},{192,128},{1,193},{65,1},{129,65},{193,129... | collective-permute-start | bytes 786440 | tf_op jit(solution)/shard_map/ppermute | solution.py:476
  87.3 16.7 %collective-permute-start.8 = (f32[4,2,128,256]{3,2,1,0:T(8,128)S(1)}, f32[4,2,128,256]{3,2,1,0:T(8,128)S(1)}, u32[]{:S(2)}, u32[]{:S(2)}) collective-permute-start(f32[4,2,128,256]{3,2,1,0:T(8,128)S(1)} %all_to_all.10), channel_id=1, source_target_pairs={{1,0},{2,1},{3,2},{4,3},{5,4},{6,5},{7,6},{8,7},{9,8},{10,9},{11,1... | collective-permute-start | bytes 3145736 | tf_op jit(solution)/shard_map/ppermute | solution.py:512
  91.7 18.2 %collective-permute-start.7 = (f32[4,2,128,256]{3,2,1,0:T(8,128)S(1)}, f32[4,2,128,256]{3,2,1,0:T(8,128)S(1)}, u32[]{:S(2)}, u32[]{:S(2)}) collective-permute-start(f32[4,2,128,256]{3,2,1,0:T(8,128)S(1)} %all_to_all.10), channel_id=1, source_target_pairs={{0,1},{1,2},{2,3},{3,4},{4,5},{5,6},{6,7},{7,8},{8,9},{9,10},{10,1... | collective-permute-start | bytes 3145736 | tf_op jit(solution)/shard_map/ppermute | solution.py:511
  93.6 17.5 %collective-permute-start.9 = (f32[2,128,256]{2,1,0:T(8,128)S(1)}, f32[2,128,256]{2,1,0:T(8,128)S(1)}, u32[]{:S(2)}, u32[]{:S(2)}) collective-permute-start(f32[2,128,256]{2,1,0:T(8,128)S(1)} %get-tuple-element.40), channel_id=1, source_target_pairs={{0,64},{64,128},{128,192},{192,0},{1,65},{65,129},{129,193},{193,1... | collective-permute-start | bytes 786440 | tf_op jit(solution)/shard_map/ppermute | solution.py:476
  94.3 16.9 %collective-permute-start.10 = (f32[2,128,256]{2,1,0:T(8,128)S(1)}, f32[2,128,256]{2,1,0:T(8,128)S(1)}, u32[]{:S(2)}, u32[]{:S(2)}) collective-permute-start(f32[2,128,256]{2,1,0:T(8,128)S(1)} %get-tuple-element.41), channel_id=1, source_target_pairs={{0,128},{64,192},{128,0},{192,64},{1,129},{65,193},{129,1},{193,65... | collective-permute-start | bytes 786440 | tf_op jit(solution)/shard_map/ppermute | solution.py:476
  96.4 14.8 %collective-permute-start.11 = (f32[2,128,256]{2,1,0:T(8,128)S(1)}, f32[2,128,256]{2,1,0:T(8,128)S(1)}, u32[]{:S(2)}, u32[]{:S(2)}) collective-permute-start(f32[2,128,256]{2,1,0:T(8,128)S(1)} %get-tuple-element.42), channel_id=1, source_target_pairs={{0,192},{64,0},{128,64},{192,128},{1,193},{65,1},{129,65},{193,129... | collective-permute-start | bytes 786440 | tf_op jit(solution)/shard_map/ppermute | solution.py:476

commit v2 on v1

--- a/solution.py
+++ b/solution.py
@@ -49,15 +49,15 @@
     return np.stack(parts).reshape(5, 4, half, half)
 
 
-def cut_own(slot, object_slab, columns, width):
-    count = columns.shape[0]
+def cut_own(here, object_slab, positions, width):
+    count = positions.shape[0]
     planes, rows, _ = object_slab.shape
 
-    def body(slot_ref, columns_ref, slab_ref, *refs):
+    def body(here_ref, positions_ref, slab_ref, *refs):
         sems = refs[count]
         copies = []
         for k in range(count):
-            start = pl.multiple_of(columns_ref[lax.rem(slot_ref[0] + k, count)], 128)
+            start = pl.multiple_of(positions_ref[lax.rem(here_ref[0] + k, count), 1], 128)
             copies.append(
                 pltpu.make_async_copy(slab_ref.at[:, :, pl.ds(start, width)], refs[k], sems.at[k])
             )
@@ -74,18 +74,18 @@
         scratch_shapes=[pltpu.SemaphoreType.DMA((count,))],
         compiler_params=SMALL,
         name="cut_own",
-    )(slot, columns, off_chip(object_slab))
-
-
-def cut_rims(object_slab, above, below, width):
-    count = above.shape[0]
+    )(here, positions, off_chip(object_slab))
+
+
+def cut_rims(object_slab, outer, inner, width):
+    count = outer.shape[0]
     planes, rows, _ = object_slab.shape
 
-    def body(above_ref, below_ref, slab_ref, for_above, for_below, sems):
+    def body(outer_ref, inner_ref, slab_ref, for_outer, for_inner, sems):
         copies = []
-        for side, (places_ref, target) in enumerate(((above_ref, for_above), (below_ref, for_below))):
+        for side, (positions_ref, target) in enumerate(((outer_ref, for_outer), (inner_ref, for_inner))):
             for k in range(count):
-                start = pl.multiple_of(places_ref[k, 1], 128)
+                start = pl.multiple_of(positions_ref[k, 1], 128)
                 copies.append(
                     pltpu.make_async_copy(
                         slab_ref.at[:, :, pl.ds(start, width)], target.at[k], sems.at[side, k]
@@ -104,25 +104,35 @@
         scratch_shapes=[pltpu.SemaphoreType.DMA((2, count))],
         compiler_params=SMALL,
         name="cut_rims",
-    )(above, below, off_chip(object_slab))
-
-
-def blend(places, from_above, from_below):
-    count, planes, rows, width = from_above.shape
-
-    def body(places_ref, above_ref, below_ref, out_ref):
+    )(outer, inner, off_chip(object_slab))
+
+
+def blend(here, positions, from_outer, from_inner):
+    count, planes, rows, width = from_outer.shape
+
+    def body(here_ref, positions_ref, outer_ref, inner_ref, *out_refs):
         row = lax.broadcasted_iota(jnp.int32, (planes, rows, width), 1)
-        for k in range(count):
-            out_ref[k] = jnp.where(row < places_ref[k, 0], below_ref[k], above_ref[k])
-
-    return pl.pallas_call(
-        body,
-        out_shape=on_chip(from_above.shape),
-        in_specs=[SMEM, VMEM, VMEM],
-        out_specs=VMEM,
+        owner = here_ref[1]
+        for shift in range(count):
+            k = lax.rem(here_ref[0] + shift, count)
+            edge = positions_ref[k, 0] - (owner - 1) * rows
+
+            @pl.when(lax.rem(owner, 2) == 1)
+            def _():
+                out_refs[shift][...] = jnp.where(row < edge, outer_ref[k], inner_ref[k])
+
+            @pl.when(lax.rem(owner, 2) == 0)
+            def _():
+                out_refs[shift][...] = jnp.where(row < edge, inner_ref[k], outer_ref[k])
+
+    return pl.pallas_call(
+        body,
+        out_shape=[on_chip((planes, rows, width))] * count,
+        in_specs=[SMEM, SMEM, VMEM, VMEM],
+        out_specs=[VMEM] * count,
         compiler_params=SMALL,
         name="blend",
-    )(places, chip(from_above), chip(from_below))
+    )(here, positions, chip(from_outer), chip(from_inner))
 
 
 def split(value):
@@ -204,26 +214,33 @@
     )(control, probe, off_chip(intensity), tables)
 
 
-def chain(control, owns, halo, left, right, start, measured):
-    slices, _, half, size = halo.shape
+def chain(control, owns, halos, left, right, start, measured):
+    slices = len(owns)
+    _, half, size = owns[0].shape
+    shape = (slices, 2, half, size)
     low_part = jnp.bfloat16
 
     def body(*refs):
-        control_ref, *own_parts = refs[: slices + 1]
-        halo_ref, left_hbm, right_hbm, start_hbm, measured_hbm = refs[slices + 1 : slices + 6]
-        grad_parts = refs[slices + 6 : 2 * slices + 6]
-        grad_halo, own_ref, grad_own, waves, adjoint, stack, rows, left_ref, right_ref, measured_ref = refs[
-            2 * slices + 6 : 2 * slices + 16
+        control_ref, *parts = refs[: 2 * slices + 1]
+        refs = refs[2 * slices + 1 :]
+        left_hbm, right_hbm, start_hbm, measured_hbm = refs[:4]
+        grad_parts = refs[4 : slices + 4]
+        grad_halo, own_ref, halo_ref, grad_own, waves, adjoint, stack, rows, left_ref, right_ref, measured_ref = refs[
+            slices + 4 : slices + 15
         ]
-        sems, own_sems, grad_sems = refs[2 * slices + 16 :]
+        sems, own_sems, halo_sems, grad_sems = refs[slices + 15 :]
         live = control_ref[0]
         slot = control_ref[1]
-        arrivals = [
-            pltpu.make_async_copy(
-                own_parts[shift], own_ref.at[lax.rem(slot + slices - shift, slices)], own_sems.at[shift]
+
+        def arrivals(shift, index):
+            return (
+                pltpu.make_async_copy(parts[shift], own_ref.at[index], own_sems.at[index]),
+                pltpu.make_async_copy(parts[slices + shift], halo_ref.at[index], halo_sems.at[index]),
             )
-            for shift in range(slices)
-        ]
+
+        def arrive(index):
+            for copy in arrivals(0, index):
+                copy.wait()
 
         def departure(shift):
             return pltpu.make_async_copy(
@@ -324,16 +341,21 @@
 
         @pl.when(live != 0)
         def _():
-            for copy in arrivals + first + later:
+            for shift in range(slices):
+                for copy in arrivals(shift, lax.rem(slot + slices - shift, slices)):
+                    copy.start()
+            for copy in first + later:
                 copy.start()
-            for copy in arrivals + first:
+            for copy in first:
                 copy.wait()
 
             @pl.loop(0, slices - 1)
             def _(index):
+                arrive(index)
                 modulate(index, waves, index)
                 unmix(*sandwich((0, 1), (0, 1), True), keep(waves, index + 1))
 
+            arrive(slices - 1)
             modulate(slices - 1, waves, slices - 1)
             for copy in later:
                 copy.wait()
@@ -365,12 +387,13 @@
 
     return pl.pallas_call(
         body,
-        out_shape=[jax.ShapeDtypeStruct(halo.shape[1:], jnp.float32)] * slices + [on_chip(halo.shape)],
-        in_specs=[SMEM] + [ANY] * slices + [VMEM] + [HBM] * 4,
+        out_shape=[jax.ShapeDtypeStruct(shape[1:], jnp.float32)] * slices + [on_chip(shape)],
+        in_specs=[SMEM] + [ANY] * (2 * slices) + [HBM] * 4,
         out_specs=[HBM] * slices + [VMEM],
         scratch_shapes=[
-            pltpu.VMEM(halo.shape, jnp.float32),
-            pltpu.VMEM(halo.shape, jnp.float32),
+            pltpu.VMEM(shape, jnp.float32),
+            pltpu.VMEM(shape, jnp.float32),
+            pltpu.VMEM(shape, jnp.float32),
             pltpu.VMEM((slices, 2, size, size), jnp.float32),
             pltpu.VMEM((1, 2, size, size), jnp.float32),
             pltpu.VMEM((2, 3 * size, size), low_part),
@@ -381,38 +404,54 @@
             pltpu.SemaphoreType.DMA((6,)),
             pltpu.SemaphoreType.DMA((slices,)),
             pltpu.SemaphoreType.DMA((slices,)),
+            pltpu.SemaphoreType.DMA((slices,)),
         ],
         compiler_params=SMALL,
         name="chain",
     )(
         control,
         *owns,
-        chip(halo),
+        *halos,
         *[off_chip(value) for value in (left, right, start, measured)],
     )
 
 
-def gather_rims(above, below, from_above, from_below, width):
-    count, planes, strip, size = from_above.shape
-
-    def body(places_above, places_below, above_ref, below_ref, out_ref):
+def gather_rims(here, outer, inner, from_outer, from_inner, width):
+    count, planes, strip, size = from_outer.shape
+
+    def body(here_ref, outer_places, inner_places, outer_ref, inner_ref, out_ref):
+        owner = here_ref[1]
         row = lax.broadcasted_iota(jnp.int32, (planes, strip, size), 1)
         out_ref[...] = jnp.zeros_like(out_ref)
-        for places_ref, ref, upper in ((places_above, above_ref, True), (places_below, below_ref, False)):
+
+        def add(places_ref, ref, upper):
             for k in range(count):
                 start = pl.multiple_of(places_ref[k, 1], 128)
-                mask = row < places_ref[k, 0] if upper else row >= places_ref[k, 0]
+                if upper:
+                    mask = row < places_ref[k, 0] - (owner - 2) * strip
+                else:
+                    mask = row >= places_ref[k, 0] - owner * strip
                 at = (slice(None), slice(None), pl.ds(start, size))
                 out_ref[at] = out_ref[at] + jnp.where(mask, ref[k], 0.0)
 
+        @pl.when(lax.rem(owner, 2) == 1)
+        def _():
+            add(inner_places, inner_ref, True)
+            add(outer_places, outer_ref, False)
+
+        @pl.when(lax.rem(owner, 2) == 0)
+        def _():
+            add(outer_places, outer_ref, True)
+            add(inner_places, inner_ref, False)
+
     return pl.pallas_call(
         body,
         out_shape=on_chip((planes, strip, width)),
-        in_specs=[SMEM, SMEM, VMEM, VMEM],
+        in_specs=[SMEM] * 3 + [VMEM] * 2,
         out_specs=VMEM,
         compiler_params=SMALL,
         name="gather_rims",
-    )(above, below, chip(from_above), chip(from_below))
+    )(here, outer, inner, chip(from_outer), chip(from_inner))
 
 
 def gather_strip(slot, places, owns, rims):
@@ -453,12 +492,12 @@
     )(slot, places, chip(rims), *[chip(value) for value in owns])
 
 
-def steering(slot, counts, places, strip):
-    def body(slot_ref, counts_ref, places_ref, out_ref):
-        slot = slot_ref[0]
+def steering(here, counts, positions, strip):
+    def body(here_ref, counts_ref, positions_ref, out_ref):
+        slot = here_ref[0]
         out_ref[0] = (slot < counts_ref[0]).astype(jnp.int32)
         out_ref[1] = slot
-        out_ref[2] = strip - places_ref[slot, 0]
+        out_ref[2] = here_ref[1] * strip - positions_ref[slot, 0]
 
     return pl.pallas_call(
         body,
@@ -467,7 +506,7 @@
         out_specs=SMEM,
         compiler_params=SMALL,
         name="steering",
-    )(slot, counts, places)
+    )(here, counts, positions)
 
 
 def shifted(values):
@@ -483,37 +522,35 @@
     strip = object_slab.shape[1]
     width = object_slab.shape[2]
     size = probe.shape[-1]
-    owner = lax.axis_index("lat")
-    slot = lax.axis_index("cuts")
     owners = lax.axis_size("lat")
-    downward = [(i, i + 1) for i in range(owners - 1)]
-    upward = [(i + 1, i) for i in range(owners - 1)]
+    here = jnp.stack([lax.axis_index("cuts"), lax.axis_index("lat")])
+    outer = [(i, i + 1) for i in range(1, owners - 1, 2)]
+    outer += [(j, i) for i, j in outer]
+    inner = [(i, i + 1) for i in range(0, owners, 2)]
+    inner += [(j, i) for i, j in inner]
     tables = jnp.asarray(wave_tables(size))
 
-    edges = positions[:, 0] - (owner - 1) * strip
-    places = jnp.stack([edges, positions[:, 1]], axis=1)
-    slot = slot[None]
-    places_above = lax.ppermute(places, "lat", downward)
-    places_below = lax.ppermute(places, "lat", upward)
-    owns = cut_own(slot, object_slab, positions[:, 1], size)
-    for_above, for_below = cut_rims(object_slab, places_above, places_below, size)
-    from_below = lax.ppermute(for_above, "lat", upward)
-    from_above = lax.ppermute(for_below, "lat", downward)
+    outer_places = lax.ppermute(positions, "lat", outer)
+    inner_places = lax.ppermute(positions, "lat", inner)
+    for_outer, for_inner = cut_rims(object_slab, outer_places, inner_places, size)
+    from_outer = lax.ppermute(for_outer, "lat", outer)
+    owns = cut_own(here, object_slab, positions, size)
     owns = shifted(owns)
-    control = steering(slot, counts, places, strip)
+    from_inner = lax.ppermute(for_inner, "lat", inner)
+    control = steering(here, counts, positions, strip)
     left, right, start, measured = prepare(control, probe, intensity, tables)
-    halo = blend(places, from_above, from_below)
-    halo = lax.all_to_all(halo, "cuts", 0, 0, tiled=True)
-
-    *grad_owns, grad_halo = chain(control, owns, halo, left, right, start, measured)
+    halos = blend(here, positions, from_outer, from_inner)
+    halos = shifted(halos)
+
+    *grad_owns, grad_halo = chain(control, owns, halos, left, right, start, measured)
 
     grad_halo = lax.all_to_all(grad_halo, "cuts", 0, 0, tiled=True)
-    back_above = lax.ppermute(grad_halo, "lat", downward)
-    back_below = lax.ppermute(grad_halo, "lat", upward)
+    back_outer = lax.ppermute(grad_halo, "lat", outer)
+    back_inner = lax.ppermute(grad_halo, "lat", inner)
     grad_owns, grad_halo = lax.optimization_barrier((grad_owns, grad_halo))
     grad_owns = shifted(grad_owns)
-    rims = gather_rims(places_above, places_below, back_above, back_below, width)
-    summed = gather_strip(slot, places, grad_owns, rims)
+    rims = gather_rims(here, outer_places, inner_places, back_outer, back_inner, width)
+    summed = gather_strip(here, positions, grad_owns, rims)
     return summed[:, None]
 
 

time: 114 us -> 98.8 us (0.87)
  the two profiles are of different devices: /device:TPU:24 before, /device:TPU:8 now
where the time goes in v2:
time: 98.8 us; the launch traced here: 98.5 us
  starting transfers between devices  31 us (31%)
  Pallas kernels  24.6 us (25%)
  waiting for transfers between devices  23.8 us (24%)
  blocking collectives  17.5 us (18%)
    all_to_all x1, blocking collectives, strip_gradient(): grad_halo = lax.all_to_all(grad_halo, 'cuts', 0, 0, tiled=True)  17.5 us
    ppermute x9, starting transfers between devices, shifted(): lax.ppermute(value, 'cuts', [(i, (i + k) % count) for i in range(count)])  15 us
    ppermute x1, waiting for transfers between devices, strip_gradient(): back_outer = lax.ppermute(grad_halo, 'lat', outer)  12.3 us
    pallas_call x1, Pallas kernels, chain(): pl.pallas_call(body, out_shape=[jax.ShapeDtypeStruct(shape[1:], jnp.float...  9.43 us
    ppermute x1, starting transfers between devices, strip_gradient(): outer_places = lax.ppermute(positions, 'lat', outer)  7.75 us
    ppermute x1, starting transfers between devices, strip_gradient(): from_outer = lax.ppermute(for_outer, 'lat', outer)  5.7 us
    ppermute x9, waiting for transfers between devices, shifted(): lax.ppermute(value, 'cuts', [(i, (i + k) % count) for i in range(count)])  5.18 us
    ppermute x1, waiting for transfers between devices, strip_gradient(): from_outer = lax.ppermute(for_outer, 'lat', outer)  5.08 us
  transfers between devices with their start and end apart: 15, of which 4 were waited for; matrix products, arithmetic and copies ran while one was open for 0% of the time, Pallas kernels for 9%

profile of v2, /device:TPU:8, one launch (start us, length us, event | category | flops | bytes accessed | tf_op | source)
XLA Modules:
  0.0 98.5 jit_solution(2390114681863498024)
XLA Ops:
  0.0 0.8 copy.12.positions_ref.places_ref
  0.8 0.0 collective-permute-start.1
  0.8 7.8 %collective-permute-start = (s32[4,2]{1,0:T(4,128)S(1)}, s32[4,2]{1,0:T(4,128)S(1)}, u32[]{:S(2)}, u32[]{:S(2)}) collective-permute-start(s32[4,2]{1,0:T(4,128)S(1)} %copy.12.positions_ref.places_ref), channel_id=1, source_target_pairs={{1,2},{3,4},{5,6},{7,8},{9,10},{11,12},{13,14},{15,16},{17,18},{19... | collective-permute-start | bytes 104 | tf_op jit(solution)/shard_map/ppermute | solution.py:533
  8.5 0.0 collective-permute-done.1.inner_ref.inner_places
  8.5 1.3 %collective-permute-done.outer_ref.outer_places = s32[4,2]{1,0:T(4,128)S(1)} collective-permute-done((s32[4,2]{1,0:T(4,128)S(1)}, s32[4,2]{1,0:T(4,128)S(1)}, u32[]{:S(2)}, u32[]{:S(2)}) %collective-permute-start) | collective-permute-done | bytes 64 | tf_op jit(solution)/shard_map/ppermute | solution.py:533
  9.8 3.8 %cut_rims.1 = (f32[4,2,128,256]{3,2,1,0:T(8,128)}, f32[4,2,128,256]{3,2,1,0:T(8,128)}) custom-call(s32[4,2]{1,0:T(4,128)S(1)} %collective-permute-done.outer_ref.outer_places, s32[4,2]{1,0:T(4,128)S(1)} %collective-permute-done.1.inner_ref.inner_places, f32[2,128,4096]{2,1,0:T(8,128)} %bitcast.6), custom_call_target="tpu_custom_call" | custom-call | tf_op jit(solution)/shard_map/cut_rims/pallas_call | solution.py:99
  13.6 0.0 copy-start
  13.6 0.0 copy-start.1
  13.6 5.7 %collective-permute-start.5 = (f32[4,2,128,256]{3,2,1,0:T(8,128)}, f32[4,2,128,256]{3,2,1,0:T(8,128)S(1)}, u32[]{:S(2)}, u32[]{:S(2)}) collective-permute-start(f32[4,2,128,256]{3,2,1,0:T(8,128)} %get-tuple-element.32), channel_id=1, source_target_pairs={{1,2},{3,4},{5,6},{7,8},{9,10},{11,12},{13,14},{15,16},{17,18},{19... | collective-permute-start | bytes 3145736 | tf_op jit(solution)/shard_map/ppermute | solution.py:536
  19.3 0.1 collective-permute-start.6
  19.4 0.1 pad_add_fusion.here_ref.slot_ref
  19.5 1.9 %cut_own.1 = (f32[2,128,256]{2,1,0:T(8,128)S(1)}, f32[2,128,256]{2,1,0:T(8,128)S(1)}, f32[2,128,256]{2,1,0:T(8,128)S(1)}, f32[2,128,256]{2,1,0:T(8,128)S(1)}) custom-call(s32[2]{0:T(128)S(1)} %pad_add_fusion.here_ref.slot_ref, s32[4,2]{1,0:T(4,128)S(1)} %copy.12.positions_ref.places_ref, f32[2,128,4096]{2,1,0:T(8,128)} %bitcast.7), custom_call_target="tpu_custom_call" | custom-call | tf_op jit(solution)/shard_map/cut_own/pallas_call | solution.py:69
  21.4 1.6 %collective-permute-start.2 = (f32[2,128,256]{2,1,0:T(8,128)S(1)}, f32[2,128,256]{2,1,0:T(8,128)S(1)}, u32[]{:S(2)}, u32[]{:S(2)}) collective-permute-start(f32[2,128,256]{2,1,0:T(8,128)S(1)} %get-tuple-element.29), channel_id=1, source_target_pairs={{0,64},{64,128},{128,192},{192,0},{1,65},{65,129},{129,193},{193,1... | collective-permute-start | bytes 786440 | tf_op jit(solution)/shard_map/ppermute | solution.py:515
  22.9 2.7 %collective-permute-start.3 = (f32[2,128,256]{2,1,0:T(8,128)S(1)}, f32[2,128,256]{2,1,0:T(8,128)S(1)}, u32[]{:S(2)}, u32[]{:S(2)}) collective-permute-start(f32[2,128,256]{2,1,0:T(8,128)S(1)} %get-tuple-element.30), channel_id=1, source_target_pairs={{0,128},{64,192},{128,0},{192,64},{1,129},{65,193},{129,1},{193,65... | collective-permute-start | bytes 786440 | tf_op jit(solution)/shard_map/ppermute | solution.py:515
  25.7 1.4 %collective-permute-start.4 = (f32[2,128,256]{2,1,0:T(8,128)S(1)}, f32[2,128,256]{2,1,0:T(8,128)S(1)}, u32[]{:S(2)}, u32[]{:S(2)}) collective-permute-start(f32[2,128,256]{2,1,0:T(8,128)S(1)} %get-tuple-element.31), channel_id=1, source_target_pairs={{0,192},{64,0},{128,64},{192,128},{1,193},{65,1},{129,65},{193,129... | collective-permute-start | bytes 786440 | tf_op jit(solution)/shard_map/ppermute | solution.py:515
  27.1 5.1 %collective-permute-done.5.outer_ref = f32[4,2,128,256]{3,2,1,0:T(8,128)S(1)} collective-permute-done((f32[4,2,128,256]{3,2,1,0:T(8,128)}, f32[4,2,128,256]{3,2,1,0:T(8,128)S(1)}, u32[]{:S(2)}, u32[]{:S(2)}) %collective-permute-start.5) | collective-permute-done | bytes 1048608 | tf_op jit(solution)/shard_map/ppermute | solution.py:536
  32.2 0.0 collective-permute-done.6.inner_ref
  32.2 0.7 blend.1
  32.9 1.6 %collective-permute-start.7 = (f32[2,128,256]{2,1,0:T(8,128)S(1)}, f32[2,128,256]{2,1,0:T(8,128)S(1)}, u32[]{:S(2)}, u32[]{:S(2)}) collective-permute-start(f32[2,128,256]{2,1,0:T(8,128)S(1)} %get-tuple-element.35), channel_id=1, source_target_pairs={{0,64},{64,128},{128,192},{192,0},{1,65},{65,129},{129,193},{193,1... | collective-permute-start | bytes 786440 | tf_op jit(solution)/shard_map/ppermute | solution.py:515
  34.5 2.7 %collective-permute-start.8 = (f32[2,128,256]{2,1,0:T(8,128)S(1)}, f32[2,128,256]{2,1,0:T(8,128)S(1)}, u32[]{:S(2)}, u32[]{:S(2)}) collective-permute-start(f32[2,128,256]{2,1,0:T(8,128)S(1)} %get-tuple-element.36), channel_id=1, source_target_pairs={{0,128},{64,192},{128,0},{192,64},{1,129},{65,193},{129,1},{193,65... | collective-permute-start | bytes 786440 | tf_op jit(solution)/shard_map/ppermute | solution.py:515
  37.2 0.0 collective-permute-done.2.refs_2_
  37.2 1.4 %collective-permute-start.9 = (f32[2,128,256]{2,1,0:T(8,128)S(1)}, f32[2,128,256]{2,1,0:T(8,128)S(1)}, u32[]{:S(2)}, u32[]{:S(2)}) collective-permute-start(f32[2,128,256]{2,1,0:T(8,128)S(1)} %get-tuple-element.37), channel_id=1, source_target_pairs={{0,192},{64,0},{128,64},{192,128},{1,193},{65,1},{129,65},{193,129... | collective-permute-start | bytes 786440 | tf_op jit(solution)/shard_map/ppermute | solution.py:515
  39.3 1.2 %steering.1.control_ref.refs_0_ = s32[3]{0:T(128)S(1)} custom-call(s32[2]{0:T(128)S(1)} %pad_add_fusion.here_ref.slot_ref, s32[1]{0:T(128)S(6)} %copy.14.counts_ref, s32[4,2]{1,0:T(4,128)S(1)} %copy.12.positions_ref.places_ref), custom_call_target="tpu_custom_call" | custom-call | tf_op jit(solution)/shard_map/steering/pallas_call | solution.py:502
  40.5 0.0 copy-done
  40.5 0.0 copy-done.1
  40.5 3.7 %prepare.1 = (bf16[5,256,768]{2,1,0:T(8,128)(2,1)}, bf16[5,768,256]{2,1,0:T(8,128)(2,1)}, f32[2,256,256]{2,1,0:T(8,128)}, f32[256,256]{1,0:T(8,128)}) custom-call(s32[3]{0:T(128)S(1)} %steering.1.control_ref.refs_0_, f32[2,256,256]{2,1,0:T(8,128)S(1)} %copy-done.1, f32[4,256,256]{2,1,0:T(8,128)} %intensity_ref.1, bf16[5,4,128,128]{3,2,1,0:T(8,128)(2,1)S(1)} %copy-done), custom_call_target="tpu_custom_call" | custom-call | tf_op jit(solution)/shard_map/prepare/pallas_call | solution.py:196
  44.2 0.0 collective-permute-done.3.refs_3_
  44.2 0.0 collective-permute-done.4.refs_4_
  44.2 0.0 collective-permute-done.7.refs_6_
  44.3 5.2 %collective-permute-done.8.refs_7_ = f32[2,128,256]{2,1,0:T(8,128)S(1)} collective-permute-done((f32[2,128,256]{2,1,0:T(8,128)S(1)}, f32[2,128,256]{2,1,0:T(8,128)S(1)}, u32[]{:S(2)}, u32[]{:S(2)}) %collective-permute-start.8) | collective-permute-done | bytes 262176 | tf_op jit(solution)/shard_map/ppermute | solution.py:515
  49.4 0.0 collective-permute-done.9.refs_8_
  49.4 9.4 %chain.1 = (f32[2,128,256]{2,1,0:T(8,128)S(1)}, f32[2,128,256]{2,1,0:T(8,128)S(1)}, f32[2,128,256]{2,1,0:T(8,128)S(1)}, f32[2,128,256]{2,1,0:T(8,128)S(1)}, f32[4,2,128,256]{3,2,1,0:T(8,128)S(1)}) custom-call(s32[3]{0:T(128)S(1)} %steering.1.control_ref.refs_0_, f32[2,128,256]{2,1,0:T(8,128)S(1)} %get-tuple-element.28.refs_1_, ...), custom_call_target="tpu_custom_call" | custom-call | tf_op jit(solution)/shard_map/chain/pallas_call | solution.py:388
  58.9 17.5 %all_to_all.5 = f32[4,2,128,256]{3,2,1,0:T(8,128)S(1)} all-to-all(f32[4,2,128,256]{3,2,1,0:T(8,128)S(1)} %get-tuple-element.42), channel_id=1, replica_groups=mesh['cuts'=4,'lat'=64] {'cuts'}, dimensions={0} | all-to-all | bytes 2097152 | tf_op jit(solution)/shard_map/all_to_all | solution.py:547
  76.4 0.0 collective-permute-start.11
  76.4 2.4 %collective-permute-start.10 = (f32[4,2,128,256]{3,2,1,0:T(8,128)S(1)}, f32[4,2,128,256]{3,2,1,0:T(8,128)S(1)}, u32[]{:S(2)}, u32[]{:S(2)}) collective-permute-start(f32[4,2,128,256]{3,2,1,0:T(8,128)S(1)} %all_to_all.5), channel_id=1, source_target_pairs={{1,2},{3,4},{5,6},{7,8},{9,10},{11,12},{13,14},{15,16},{17,18},{19... | collective-permute-start | bytes 3145736 | tf_op jit(solution)/shard_map/ppermute | solution.py:548
  78.8 0.6 collective-permute-start.12
  79.4 2.1 %collective-permute-start.13 = (f32[2,128,256]{2,1,0:T(8,128)S(1)}, f32[2,128,256]{2,1,0:T(8,128)S(1)}, u32[]{:S(2)}, u32[]{:S(2)}) collective-permute-start(f32[2,128,256]{2,1,0:T(8,128)S(1)} %get-tuple-element.49), channel_id=1, source_target_pairs={{0,128},{64,192},{128,0},{192,64},{1,129},{65,193},{129,1},{193,65... | collective-permute-start | bytes 786440 | tf_op jit(solution)/shard_map/ppermute | solution.py:515
  81.5 0.8 collective-permute-start.14
  82.3 0.0 collective-permute-done.11.inner_ref
  82.3 12.3 %collective-permute-done.10.outer_ref = f32[4,2,128,256]{3,2,1,0:T(8,128)S(1)} collective-permute-done((f32[4,2,128,256]{3,2,1,0:T(8,128)S(1)}, f32[4,2,128,256]{3,2,1,0:T(8,128)S(1)}, u32[]{:S(2)}, u32[]{:S(2)}) %collective-permute-start.10) | collective-permute-done | bytes 1048608 | tf_op jit(solution)/shard_map/ppermute | solution.py:548
  94.6 1.2 %gather_rims.1.rims_ref = f32[2,128,4096]{2,1,0:T(8,128)S(1)} custom-call(s32[2]{0:T(128)S(1)} %pad_add_fusion.here_ref.slot_ref, s32[4,2]{1,0:T(4,128)S(1)} %collective-permute-done.outer_ref.outer_places, s32[4,2]{1,0:T(4,128)S(1)} %collective-permute-done.1.inner_ref.inner_places, f32[4,2,128,256]{3,2,1,0:T(8,128)S(1)} %collective-permute-done.10.outer_ref, ...), custom_call_target="tpu_custom_call" | custom-call | tf_op jit(solution)/shard_map/gather_rims/pallas_call | solution.py:447
  95.8 0.0 collective-permute-done.12.refs_1_
  95.8 0.0 collective-permute-done.13.refs_2_
  95.8 0.0 collective-permute-done.14.refs_3_
  95.8 2.7 %gather_strip.1 = f32[2,128,4096]{2,1,0:T(8,128)} custom-call(s32[2]{0:T(128)S(1)} %pad_add_fusion.here_ref.slot_ref, s32[4,2]{1,0:T(4,128)S(1)} %copy.12.positions_ref.places_ref, f32[2,128,4096]{2,1,0:T(8,128)S(1)} %gather_rims.1.rims_ref, f32[2,128,256]{2,1,0:T(8,128)S(1)} %get-tuple-element.47.refs_0_, ...), custom_call_target="tpu_custom_call" | custom-call | tf_op jit(solution)/shard_map/gather_strip/pallas_call | solution.py:481
Async XLA Ops:
  0.8 7.8 %collective-permute-start.1 = (s32[4,2]{1,0:T(4,128)S(1)}, s32[4,2]{1,0:T(4,128)S(1)}, u32[]{:S(2)}, u32[]{:S(2)}) collective-permute-start(s32[4,2]{1,0:T(4,128)S(1)} %copy.12.positions_ref.places_ref), channel_id=1, source_target_pairs={{0,1},{2,3},{4,5},{6,7},{8,9},{10,11},{12,13},{14,15},{16,17},{18,... | collective-permute-start | bytes 104 | tf_op jit(solution)/shard_map/ppermute | solution.py:534
  0.8 9.0 %collective-permute-start = (s32[4,2]{1,0:T(4,128)S(1)}, s32[4,2]{1,0:T(4,128)S(1)}, u32[]{:S(2)}, u32[]{:S(2)}) collective-permute-start(s32[4,2]{1,0:T(4,128)S(1)} %copy.12.positions_ref.places_ref), channel_id=1, source_target_pairs={{1,2},{3,4},{5,6},{7,8},{9,10},{11,12},{13,14},{15,16},{17,18},{19... | collective-permute-start | bytes 104 | tf_op jit(solution)/shard_map/ppermute | solution.py:533
  13.6 26.9 %copy-start = (bf16[5,4,128,128]{3,2,1,0:T(8,128)(2,1)S(1)}, bf16[5,4,128,128]{3,2,1,0:T(8,128)(2,1)}, u32[]{:S(2)}) copy-start(bf16[5,4,128,128]{3,2,1,0:T(8,128)(2,1)} %constant.11.clone.tables_ref) | copy-start | bytes 1966084
  13.6 26.9 %copy-start.1 = (f32[2,256,256]{2,1,0:T(8,128)S(1)}, f32[2,256,256]{2,1,0:T(8,128)}, u32[]{:S(2)}) copy-start(f32[2,256,256]{2,1,0:T(8,128)} %probe_ref.1) | copy-start | bytes 1572868
  13.6 18.6 %collective-permute-start.5 = (f32[4,2,128,256]{3,2,1,0:T(8,128)}, f32[4,2,128,256]{3,2,1,0:T(8,128)S(1)}, u32[]{:S(2)}, u32[]{:S(2)}) collective-permute-start(f32[4,2,128,256]{3,2,1,0:T(8,128)} %get-tuple-element.32), channel_id=1, source_target_pairs={{1,2},{3,4},{5,6},{7,8},{9,10},{11,12},{13,14},{15,16},{17,18},{19... | collective-permute-start | bytes 3145736 | tf_op jit(solution)/shard_map/ppermute | solution.py:536
  19.3 12.9 %collective-permute-start.6 = (f32[4,2,128,256]{3,2,1,0:T(8,128)}, f32[4,2,128,256]{3,2,1,0:T(8,128)S(1)}, u32[]{:S(2)}, u32[]{:S(2)}) collective-permute-start(f32[4,2,128,256]{3,2,1,0:T(8,128)} %get-tuple-element.33), channel_id=1, source_target_pairs={{0,1},{2,3},{4,5},{6,7},{8,9},{10,11},{12,13},{14,15},{16,17},{18,... | collective-permute-start | bytes 3145736 | tf_op jit(solution)/shard_map/ppermute | solution.py:539
  21.4 15.9 %collective-permute-start.2 = (f32[2,128,256]{2,1,0:T(8,128)S(1)}, f32[2,128,256]{2,1,0:T(8,128)S(1)}, u32[]{:S(2)}, u32[]{:S(2)}) collective-permute-start(f32[2,128,256]{2,1,0:T(8,128)S(1)} %get-tuple-element.29), channel_id=1, source_target_pairs={{0,64},{64,128},{128,192},{192,0},{1,65},{65,129},{129,193},{193,1... | collective-permute-start | bytes 786440 | tf_op jit(solution)/shard_map/ppermute | solution.py:515
  22.9 21.3 %collective-permute-start.3 = (f32[2,128,256]{2,1,0:T(8,128)S(1)}, f32[2,128,256]{2,1,0:T(8,128)S(1)}, u32[]{:S(2)}, u32[]{:S(2)}) collective-permute-start(f32[2,128,256]{2,1,0:T(8,128)S(1)} %get-tuple-element.30), channel_id=1, source_target_pairs={{0,128},{64,192},{128,0},{192,64},{1,129},{65,193},{129,1},{193,65... | collective-permute-start | bytes 786440 | tf_op jit(solution)/shard_map/ppermute | solution.py:515
  25.7 18.6 %collective-permute-start.4 = (f32[2,128,256]{2,1,0:T(8,128)S(1)}, f32[2,128,256]{2,1,0:T(8,128)S(1)}, u32[]{:S(2)}, u32[]{:S(2)}) collective-permute-start(f32[2,128,256]{2,1,0:T(8,128)S(1)} %get-tuple-element.31), channel_id=1, source_target_pairs={{0,192},{64,0},{128,64},{192,128},{1,193},{65,1},{129,65},{193,129... | collective-permute-start | bytes 786440 | tf_op jit(solution)/shard_map/ppermute | solution.py:515
  32.9 11.3 %collective-permute-start.7 = (f32[2,128,256]{2,1,0:T(8,128)S(1)}, f32[2,128,256]{2,1,0:T(8,128)S(1)}, u32[]{:S(2)}, u32[]{:S(2)}) collective-permute-start(f32[2,128,256]{2,1,0:T(8,128)S(1)} %get-tuple-element.35), channel_id=1, source_target_pairs={{0,64},{64,128},{128,192},{192,0},{1,65},{65,129},{129,193},{193,1... | collective-permute-start | bytes 786440 | tf_op jit(solution)/shard_map/ppermute | solution.py:515
  34.5 14.9 %collective-permute-start.8 = (f32[2,128,256]{2,1,0:T(8,128)S(1)}, f32[2,128,256]{2,1,0:T(8,128)S(1)}, u32[]{:S(2)}, u32[]{:S(2)}) collective-permute-start(f32[2,128,256]{2,1,0:T(8,128)S(1)} %get-tuple-element.36), channel_id=1, source_target_pairs={{0,128},{64,192},{128,0},{192,64},{1,129},{65,193},{129,1},{193,65... | collective-permute-start | bytes 786440 | tf_op jit(solution)/shard_map/ppermute | solution.py:515
  37.2 12.2 %collective-permute-start.9 = (f32[2,128,256]{2,1,0:T(8,128)S(1)}, f32[2,128,256]{2,1,0:T(8,128)S(1)}, u32[]{:S(2)}, u32[]{:S(2)}) collective-permute-start(f32[2,128,256]{2,1,0:T(8,128)S(1)} %get-tuple-element.37), channel_id=1, source_target_pairs={{0,192},{64,0},{128,64},{192,128},{1,193},{65,1},{129,65},{193,129... | collective-permute-start | bytes 786440 | tf_op jit(solution)/shard_map/ppermute | solution.py:515
  76.4 6.0 %collective-permute-start.11 = (f32[4,2,128,256]{3,2,1,0:T(8,128)S(1)}, f32[4,2,128,256]{3,2,1,0:T(8,128)S(1)}, u32[]{:S(2)}, u32[]{:S(2)}) collective-permute-start(f32[4,2,128,256]{3,2,1,0:T(8,128)S(1)} %all_to_all.5), channel_id=1, source_target_pairs={{0,1},{2,3},{4,5},{6,7},{8,9},{10,11},{12,13},{14,15},{16,17},{18,... | collective-permute-start | bytes 3145736 | tf_op jit(solution)/shard_map/ppermute | solution.py:549
  76.4 18.2 %collective-permute-start.10 = (f32[4,2,128,256]{3,2,1,0:T(8,128)S(1)}, f32[4,2,128,256]{3,2,1,0:T(8,128)S(1)}, u32[]{:S(2)}, u32[]{:S(2)}) collective-permute-start(f32[4,2,128,256]{3,2,1,0:T(8,128)S(1)} %all_to_all.5), channel_id=1, source_target_pairs={{1,2},{3,4},{5,6},{7,8},{9,10},{11,12},{13,14},{15,16},{17,18},{19... | collective-permute-start | bytes 3145736 | tf_op jit(solution)/shard_map/ppermute | solution.py:548
  78.8 17.0 %collective-permute-start.12 = (f32[2,128,256]{2,1,0:T(8,128)S(1)}, f32[2,128,256]{2,1,0:T(8,128)S(1)}, u32[]{:S(2)}, u32[]{:S(2)}) collective-permute-start(f32[2,128,256]{2,1,0:T(8,128)S(1)} %get-tuple-element.48), channel_id=1, source_target_pairs={{0,64},{64,128},{128,192},{192,0},{1,65},{65,129},{129,193},{193,1... | collective-permute-start | bytes 786440 | tf_op jit(solution)/shard_map/ppermute | solution.py:515
  79.4 16.4 %collective-permute-start.13 = (f32[2,128,256]{2,1,0:T(8,128)S(1)}, f32[2,128,256]{2,1,0:T(8,128)S(1)}, u32[]{:S(2)}, u32[]{:S(2)}) collective-permute-start(f32[2,128,256]{2,1,0:T(8,128)S(1)} %get-tuple-element.49), channel_id=1, source_target_pairs={{0,128},{64,192},{128,0},{192,64},{1,129},{65,193},{129,1},{193,65... | collective-permute-start | bytes 786440 | tf_op jit(solution)/shard_map/ppermute | solution.py:515
  81.5 14.3 %collective-permute-start.14 = (f32[2,128,256]{2,1,0:T(8,128)S(1)}, f32[2,128,256]{2,1,0:T(8,128)S(1)}, u32[]{:S(2)}, u32[]{:S(2)}) collective-permute-start(f32[2,128,256]{2,1,0:T(8,128)S(1)} %get-tuple-element.50), channel_id=1, source_target_pairs={{0,192},{64,0},{128,64},{192,128},{1,193},{65,1},{129,65},{193,129... | collective-permute-start | bytes 786440 | tf_op jit(solution)/shard_map/ppermute | solution.py:515
